TPU v7x, 512 devices: a whole 4x8x8 slice. The times are simulated.
512 devices in a mesh: ka: 16 (over y_lo, z), grid: 32 (over x, y_hi, core).
Axes of the slice: x: 4, y: 8 (y_hi: 4, y_lo: 2; y = y_hi * 2 + y_lo), z: 8, core: 2. Of those that a mesh axis runs over, the one named last changes fastest.
Arguments:
- orbitals: bfloat16 [16, 2, 32768, 256], P('ka', None, 'grid'), may hold values from -0.4453125 to 0.4453125
- fields: bfloat16 [2, 3, 2, 32768], P(None, None, None, 'grid'), may hold values from -6 to 6
- partner: int32 [2, 16], replicated, may hold values from 0 to 15, each once within a row
Outputs:
- coupling: float32 [256, 2, 3, 2, 16, 256], P('grid', None, None, None, 'ka')
Inputs may be any that keep to these rules, and one draw needn't show every extreme that they name: Each row of partner names every k-point once.
All inputs are finite; a program needn't handle non-finite values.
Results may differ from a plain program's by a relative error of at most 0.0029.
Values may be sent and summed in bfloat16 or wider, within the bound.
No kernel may reach another device: no remote copies, remote signals or barrier semaphores. Data moves between devices by JAX's collectives and lax.ppermute only.
A program may use at most 64 MiB of HBM per device.

v0:
```python
import jax
import jax.numpy as jnp
from jax import lax
from jax.sharding import PartitionSpec as P


def weigh_orbitals(field_pair, own):
    field_real = field_pair[:, 0, :].astype(jnp.float32).T
    field_imag = field_pair[:, 1, :].astype(jnp.float32).T
    own_real = own[0].astype(jnp.float32)[:, None, :]
    own_imag = own[1].astype(jnp.float32)[:, None, :]
    part_real = field_real[:, :, None] * own_real - field_imag[:, :, None] * own_imag
    part_imag = field_real[:, :, None] * own_imag + field_imag[:, :, None] * own_real
    weighted = jnp.stack([part_real, part_imag], axis=1).astype(jnp.bfloat16)
    return weighted.reshape(weighted.shape[0], -1)


def couple_block(fetched_rows, weighted, modes, bands):
    row_count = fetched_rows.shape[2]
    stacked = jnp.concatenate([fetched_rows[0], fetched_rows[1]], axis=1)
    product = lax.dot_general(
        stacked, weighted, (((0,), (0,)), ((), ())), preferred_element_type=jnp.float32
    )
    product = product.reshape(2, row_count, 2, modes, bands)
    part_real = product[0, :, 0] + product[1, :, 1]
    part_imag = product[0, :, 1] - product[1, :, 0]
    return jnp.stack([part_real, part_imag], axis=2)


def per_device(orbitals, fields, partner):
    num_q = fields.shape[0]
    modes = fields.shape[1]
    bands = orbitals.shape[3]
    fetched_list = []
    for which in range(num_q):
        picked = jnp.take(
            lax.all_to_all(orbitals, "ka", split_axis=2, concat_axis=0, tiled=True),
            partner[which],
            axis=0,
        )
        fetched_list.append(lax.all_to_all(picked, "ka", split_axis=0, concat_axis=2, tiled=True))
    weighted_list = [[weigh_orbitals(fields[which], orbitals[0])] for which in range(num_q)]
    local_rows = bands // lax.axis_size("grid")
    per_q = []
    for term_which in range(num_q):
        fetched_rows = fetched_list[term_which][0]
        per_point = [couple_block(fetched_rows, weighted_list[term_which][0], modes, bands)]
        per_q.append(jnp.stack(per_point, axis=3))
    whole = jnp.stack(per_q, axis=1)
    summed = lax.psum(whole, "grid")
    return lax.dynamic_slice_in_dim(summed, lax.axis_index("grid") * local_rows, local_rows, 0)


def solution(mesh):
    placed = (P("ka", None, "grid", None), P(None, None, None, "grid"), P())
    return jax.shard_map(
        per_device,
        mesh=mesh,
        in_specs=placed,
        out_specs=P("grid", None, None, None, "ka", None),
        check_vma=False,
    )
```

profile of v0, /device:TPU:1, one launch (start us, length us, event | category | flops | bytes accessed | tf_op | source)
XLA Modules:
  0.0 436.7 jit_solution(18288452309900060642)
XLA Ops:
  6.5 3.3 copy.27
  9.9 12.0 %all-to-all-start = ((bf16[1,2,1024,256]{3,1,0,2:T(2,128)(2,1)}), bf16[1,2,1024,256]{3,1,0,2:T(2,128)(2,1)S(1)}, u32[]{:S(2)}, u32[]{:S(2)}) async-start(bf16[1,2,1024,256]{3,1,0,2:T(2,128)(2,1)} %copy.27), calls=%async_computation | async-start | bytes 2097152 | tf_op jit(solution)/shard_map/all_to_all | solution.py:37
  21.9 25.3 %all-to-all-done = bf16[1,2,1024,256]{3,1,0,2:T(2,128)(2,1)S(1)} async-done(((bf16[1,2,1024,256]{3,1,0,2:T(2,128)(2,1)}), bf16[1,2,1024,256]{3,1,0,2:T(2,128)(2,1)S(1)}, u32[]{:S(2)}, u32[]{:S(2)}) %all-to-all-start) | async-done | bytes 1048608 | tf_op jit(solution)/shard_map/all_to_all | solution.py:37
  47.4 0.6 gather_fusion.1
  48.0 1.2 broadcast_select_fusion
  49.1 7.3 %all-to-all-start.2 = ((bf16[16,2,64,256]{3,2,1,0:T(8,128)(2,1)}), bf16[16,2,64,256]{3,2,1,0:T(8,128)(2,1)}, u32[]{:S(2)}, u32[]{:S(2)}) async-start(bf16[16,2,64,256]{3,2,1,0:T(8,128)(2,1)} %broadcast_select_fusion), calls=%async_computation.2 | async-start | bytes 2097152 | tf_op jit(solution)/shard_map/all_to_all | solution.py:41
  56.5 0.6 gather_fusion
  57.1 1.2 broadcast_select_fusion.1
  58.3 23.6 %all-to-all-done.2 = bf16[16,2,64,256]{3,2,1,0:T(8,128)(2,1)} async-done(((bf16[16,2,64,256]{3,2,1,0:T(8,128)(2,1)}), bf16[16,2,64,256]{3,2,1,0:T(8,128)(2,1)}, u32[]{:S(2)}, u32[]{:S(2)}) %all-to-all-start.2) | async-done | bytes 1048608 | tf_op jit(solution)/shard_map/all_to_all | solution.py:41
  81.9 7.2 %all-to-all-start.1 = ((bf16[16,2,64,256]{3,2,1,0:T(8,128)(2,1)}), bf16[16,2,64,256]{3,2,1,0:T(8,128)(2,1)}, u32[]{:S(2)}, u32[]{:S(2)}) async-start(bf16[16,2,64,256]{3,2,1,0:T(8,128)(2,1)} %broadcast_select_fusion.1), calls=%async_computation.1 | async-start | bytes 2097152 | tf_op jit(solution)/shard_map/all_to_all | solution.py:41
  90.2 4.0 subtract_convert_fusion.1
  94.2 1.3 fusion.13
  95.6 1.3 copy.33
  96.9 17.8 %all-to-all-done.1 = bf16[16,2,64,256]{3,2,1,0:T(8,128)(2,1)} async-done(((bf16[16,2,64,256]{3,2,1,0:T(8,128)(2,1)}), bf16[16,2,64,256]{3,2,1,0:T(8,128)(2,1)}, u32[]{:S(2)}, u32[]{:S(2)}) %all-to-all-start.1) | async-done | bytes 1048608 | tf_op jit(solution)/shard_map/all_to_all | solution.py:41
  114.7 1.4 fusion.12
  116.2 1.4 copy.30
  117.6 3.6 fusion
  121.4 1.2 copy-done.1
  122.5 0.5 copy-done.2
  123.3 1.8 fusion.3
  125.6 2.1 pad_maximum_fusion
  127.7 300.5 %all-reduce.2.cloned.1.call-done = f32[256,2,3,2,1,256]{5,0,2,3,4,1:T(8,128)} async-done(((f32[256,2,3,2,1,256]{5,0,2,3,4,1:T(8,128)}), f32[256,2,3,2,1,256]{5,0,2,3,4,1:T(8,128)}) %all-reduce.2.cloned.1.call-update) | async-done | bytes 3145744 | tf_op jit(solution)/shard_map/psum | solution.py:50
  428.2 0.9 constant_dynamic-slice_fusion
  429.1 0.7 copy.34
  (33 shorter events, 2.3 us)
Async XLA Ops:
  6.5 15.3 %copy-start.6 = (s32[2,16]{1,0:T(2,128)S(1)}, s32[2,16]{1,0:T(2,128)}, u32[]{:S(2)}) copy-start(s32[2,16]{1,0:T(2,128)} %param.7) | copy-start | bytes 388
  9.9 37.3 %all-to-all-start = ((bf16[1,2,1024,256]{3,1,0,2:T(2,128)(2,1)}), bf16[1,2,1024,256]{3,1,0,2:T(2,128)(2,1)S(1)}, u32[]{:S(2)}, u32[]{:S(2)}) async-start(bf16[1,2,1024,256]{3,1,0,2:T(2,128)(2,1)} %copy.27), calls=%async_computation | async-start | bytes 2097152 | tf_op jit(solution)/shard_map/all_to_all | solution.py:37
  49.1 32.8 %all-to-all-start.2 = ((bf16[16,2,64,256]{3,2,1,0:T(8,128)(2,1)}), bf16[16,2,64,256]{3,2,1,0:T(8,128)(2,1)}, u32[]{:S(2)}, u32[]{:S(2)}) async-start(bf16[16,2,64,256]{3,2,1,0:T(8,128)(2,1)} %broadcast_select_fusion), calls=%async_computation.2 | async-start | bytes 2097152 | tf_op jit(solution)/shard_map/all_to_all | solution.py:41
  56.5 32.8 %copy-start.5 = (bf16[2,3,2,1024]{3,2,1,0:T(2,128)(2,1)S(1)}, bf16[2,3,2,1024]{3,2,1,0:T(2,128)(2,1)}, u32[]{:S(2)}) copy-start(bf16[2,3,2,1024]{3,2,1,0:T(2,128)(2,1)} %param.6) | copy-start | bytes 73732
  56.5 32.9 %copy-start = (bf16[1,2,1024,256]{3,2,1,0:T(8,128)(2,1)S(1)}, bf16[1,2,1024,256]{3,2,1,0:T(8,128)(2,1)}, u32[]{:S(2)}) copy-start(bf16[1,2,1024,256]{3,2,1,0:T(8,128)(2,1)} %param.5) | copy-start | bytes 3145732
  81.9 32.7 %all-to-all-start.1 = ((bf16[16,2,64,256]{3,2,1,0:T(8,128)(2,1)}), bf16[16,2,64,256]{3,2,1,0:T(8,128)(2,1)}, u32[]{:S(2)}, u32[]{:S(2)}) async-start(bf16[16,2,64,256]{3,2,1,0:T(8,128)(2,1)} %broadcast_select_fusion.1), calls=%async_computation.1 | async-start | bytes 2097152 | tf_op jit(solution)/shard_map/all_to_all | solution.py:41
  89.2 339.0 %all-reduce.2.cloned.1.call-start = ((), (), s32[]{:S(2)}) async-start(), calls=%async_computation.3 | async-start | bytes 6291456 | tf_op jit(solution)/shard_map/psum | solution.py:50
  114.7 2.9 copy-start.3
  121.1 1.4 copy-start.1
  121.1 1.9 copy-start.2
  121.1 2.2 copy-start.4
Sparse Core Ops, SparseCore 0:
  127.8 300.3 all-reduce.1
where the time goes:
time: 437 us
  waiting for transfers between devices  367 us (84%)
  starting transfers between devices  26.5 us (6%)
  local copies, waits for them, and re-layouts  14.4 us (3%)
  between operations  13.7 us (3%)
  other arithmetic  9.41 us (2%)
  matrix products  5.38 us (1%)
    psum x1, waiting for transfers between devices, per_device(): summed = lax.psum(whole, 'grid')  301 us
    all_to_all x2, waiting for transfers between devices, per_device(): lax.all_to_all(picked, 'ka', split_axis=0, concat_axis=2, tiled=True)  41.4 us
    all_to_all x1, waiting for transfers between devices, per_device(): lax.all_to_all(orbitals, 'ka', split_axis=2, concat_axis=0, tiled=True)  25.3 us
    all_to_all x2, starting transfers between devices, per_device(): lax.all_to_all(picked, 'ka', split_axis=0, concat_axis=2, tiled=True)  14.5 us
    all_to_all x1, starting transfers between devices, per_device(): lax.all_to_all(orbitals, 'ka', split_axis=2, concat_axis=0, tiled=True)  12 us
  transfers between devices with their start and end apart: 4, of which 4 were waited for; matrix products, arithmetic and copies ran while one was open for 2% of the time, Pallas kernels for 0%

commit v1 on v0

v1 whole, which is shorter than its diff:
```python
import jax
import jax.numpy as jnp
from jax import lax
from jax.sharding import Mesh, PartitionSpec as P

KA = ("ylo", "z")
GRID = ("x", "yhi", "core")


def weigh(field_pair, own):
    modes = field_pair.shape[0]
    rows = own.shape[1]
    field_real = field_pair[:, 0, :].astype(jnp.float32).T[:, :, None]
    field_imag = field_pair[:, 1, :].astype(jnp.float32).T[:, :, None]
    own_real = own[0].astype(jnp.float32)[:, None, :]
    own_imag = own[1].astype(jnp.float32)[:, None, :]
    part_real = (field_real * own_real - field_imag * own_imag).astype(jnp.bfloat16)
    part_imag = (field_real * own_imag + field_imag * own_real).astype(jnp.bfloat16)
    upper = jnp.stack([part_real, part_imag], axis=2)
    lower = jnp.stack([part_imag, -part_real], axis=2)
    return jnp.stack([upper, lower], axis=0).reshape(2 * rows, -1)


def reduce_scatter(product):
    bands, width = product.shape
    core = lax.axis_size("core")
    xs = lax.axis_size("x")
    ys = lax.axis_size("yhi")
    keep = bands // (core * xs * ys)
    parts = product.reshape(xs, ys, core, keep, width)
    parts = lax.all_to_all(parts, "core", split_axis=2, concat_axis=2, tiled=True)
    parts = parts.sum(axis=2).astype(jnp.bfloat16)
    parts = lax.all_to_all(parts, "x", split_axis=0, concat_axis=0, tiled=True)
    parts = parts.astype(jnp.float32).sum(axis=0)
    parts = lax.all_to_all(parts, "yhi", split_axis=0, concat_axis=0, tiled=True)
    return parts.sum(axis=0)


def per_device(orbitals, fields, partner):
    num_q, modes = fields.shape[:2]
    own = orbitals[0]
    rows, bands = own.shape[1:]
    points = lax.axis_size(KA)
    flat = own.reshape(points, 2 * rows // points, bands)
    spread = lax.all_to_all(flat, KA, split_axis=0, concat_axis=0, tiled=True)
    results = []
    fetched = None
    for which in range(num_q):
        picked = spread.at[partner[which]].get(mode="promise_in_bounds")
        if fetched is not None:
            picked, fetched = lax.optimization_barrier((picked, fetched))
            results.append(finish(fetched, weighted))
        fetched = lax.all_to_all(picked, KA, split_axis=0, concat_axis=0, tiled=True)
        weighted = weigh(fields[which], own)
    results.append(finish(fetched, weighted))
    keep = results[0].shape[0]
    parts = [r.reshape(keep, modes, 2, 1, bands) for r in results]
    return jnp.stack(parts, axis=1)


def finish(fetched, weighted):
    lhs = fetched.reshape(-1, fetched.shape[-1])
    product = lax.dot_general(lhs, weighted, (((0,), (0,)), ((), ())), preferred_element_type=jnp.float32)
    return reduce_scatter(product)


def solution(mesh):
    fine = Mesh(mesh.devices.reshape(2, 8, 4, 4, 2), KA + GRID)
    return jax.shard_map(
        per_device,
        mesh=fine,
        in_specs=(P(KA, None, GRID, None), P(None, None, None, GRID), P()),
        out_specs=P(GRID, None, None, None, KA, None),
        check_vma=False,
    )
```

time: 437 us -> 243 us (0.56)
  the two profiles are of different devices: /device:TPU:1 before, /device:TPU:8 now
where the time goes in v1:
time: 243 us; the launch traced here: 241 us
  other arithmetic  103 us (42%)
  starting transfers between devices  45.5 us (19%)
  local copies, waits for them, and re-layouts  41.3 us (17%)
  waiting for transfers between devices  30.7 us (13%)
  blocking collectives  10.8 us (4%)
  matrix products  9.49 us (4%)
    another operation x4, other arithmetic, weigh(): return jnp.stack([upper, lower], axis=0).reshape(2 * rows, -1)  52.8 us
    reshape x2, local copies, waits for them, and re-layouts, weigh(): return jnp.stack([upper, lower], axis=0).reshape(2 * rows, -1)  29 us
    neg x1, other arithmetic, weigh(): lower = jnp.stack([part_imag, -part_real], axis=2)  27.1 us
    convert_element_type x1, other arithmetic, weigh(): (field_real * own_imag + field_imag * own_real).astype(jnp.bfloat16)  17.7 us
    all_to_all x2, waiting for transfers between devices, reduce_scatter(): lax.all_to_all(parts, 'yhi', split_axis=0, concat_axis=0, tiled=True)  16.6 us
    all_to_all x2, starting transfers between devices, per_device(): lax.all_to_all(picked, KA, split_axis=0, concat_axis=0, tiled=True)  16.3 us
    all_to_all x2, waiting for transfers between devices, reduce_scatter(): parts = lax.all_to_all(parts, 'x', split_axis=0, concat_axis=0, tiled=True)  14.1 us
    all_to_all x1, starting transfers between devices, per_device(): spread = lax.all_to_all(flat, KA, split_axis=0, concat_axis=0, tiled=True)  11.9 us
  transfers between devices with their start and end apart: 7, of which 4 were waited for; matrix products, arithmetic and copies ran while one was open for 57% of the time, Pallas kernels for 0%

profile of v1, /device:TPU:8, one launch (start us, length us, event | category | flops | bytes accessed | tf_op | source)
XLA Modules:
  0.0 241.2 jit_solution(12461403983158063802)
XLA Ops:
  0.0 11.9 %all-to-all-start = ((bf16[16,128,256]{2,1,0:T(8,128)(2,1)}), bf16[16,128,256]{2,1,0:T(8,128)(2,1)}, u32[]{:S(2)}, u32[]{:S(2)}) async-start(bf16[16,128,256]{2,1,0:T(8,128)(2,1)} %bitcast.63), calls=%async_computation | async-start | bytes 2097152 | tf_op jit(solution)/shard_map/all_to_all | solution.py:45
  16.2 17.7 %add_convert_fusion.1 = (bf16[1024,3,1,256]{3,2,1,0:T(2,128)(2,1)}, bf16[1024,3,1,256]{3,2,1,0:T(2,128)(2,1)}) fusion(f32[1024,256]{1,0:T(8,128)S(1)} %get-tuple-element.22, f32[1024,3]{1,0:T(8,128)S(1)} %copy.20, f32[1024,256]{1,0:T(8,128)S(1)} %get-tuple-element.21, f32[1024,3]{1,0:T(8,128)S(1)} %copy.19, f32[1024,3]{1,0:T(8,128)} %copy.24, f32[1024,3]{1,0:T(8,128)} %copy.23), kind=kLoop, calls=%fused_computation.14 | loop fusion | flops 6291456 | bytes 5292032 | tf_op jit(solution)/shard_map/convert_element_type | solution.py:18
  34.0 27.1 %fusion.8 = (bf16[1024,3,1,256]{3,2,1,0:T(2,128)(2,1)}, bf16[1024,3,1,256]{3,2,1,0:T(2,128)(2,1)}, bf16[1024,3,1,256]{3,2,1,0:T(2,128)(2,1)S(1)}, bf16[1024,3,1,256]{3,2,1,0:T(2,128)(2,1)}) fusion(f32[1024,256]{1,0:T(8,128)} %copy-done.1, f32[1024,3]{1,0:T(8,128)} %copy-done.4, f32[1024,256]{1,0:T(8,128)} %copy-done, f32[1024,3]{1,0:T(8,128)} %copy-done.3, ...), kind=kLoop, calls=%fused_computation.39 | loop fusion | flops 7864320 | bytes 8437760 | tf_op jit(solution)/shard_map/neg | solution.py:20
  61.2 2.8 %gather_fusion.1 = bf16[16,128,256]{2,1,0:T(8,128)(2,1)} fusion(bf16[16,128,256]{2,1,0:T(8,128)(2,1)} %all-to-all-done, s32[1024]{0:T(1024)S(1)} %pad_clamp_fusion), kind=kCustom, calls=%fused_computation.1 | custom fusion | bytes 2097216 | tf_op jit(solution)/shard_map/gather | solution.py:49
  64.0 8.1 %all-to-all-start.1 = ((bf16[16,128,256]{2,1,0:T(8,128)(2,1)}), bf16[16,128,256]{2,1,0:T(8,128)(2,1)}, u32[]{:S(2)}, u32[]{:S(2)}) async-start(bf16[16,128,256]{2,1,0:T(8,128)(2,1)} %gather_fusion.1), calls=%async_computation.1 | async-start | bytes 2097152 | tf_op jit(solution)/shard_map/all_to_all | solution.py:53
  72.1 16.0 %maximum_bitcast_fusion = (bf16[1,1024,3,2,256]{4,3,2,1,0:T(2,128)(2,1)S(1)}, bf16[1,1024,3,2,256]{4,3,2,1,0:T(2,128)(2,1)S(1)}) fusion(bf16[1024,3,1,256]{3,2,1,0:T(2,128)(2,1)} %get-tuple-element.17, bf16[1024,3,1,256]{3,2,1,0:T(2,128)(2,1)} %get-tuple-element.10, bf16[1024,3,1,256]{3,2,1,0:T(2,128)(2,1)} %get-tuple-element.9), kind=kLoop, calls=%fused_computation.8 | loop fusion | flops 12582912 | bytes 11010048 | tf_op jit(solution)/shard_map/stack | solution.py:21
  88.2 10.5 %pad_maximum_fusion = bf16[2,1024,3,2,256]{4,3,2,1,0:T(2,128)(2,1)} fusion(bf16[1,1024,3,2,256]{4,3,2,1,0:T(2,128)(2,1)S(1)} %get-tuple-element.14, bf16[1,1024,3,2,256]{4,3,2,1,0:T(2,128)(2,1)S(1)} %get-tuple-element.13), kind=kLoop, calls=%fused_computation.2 | loop fusion | flops 3145728 | bytes 12582912 | tf_op jit(solution)/shard_map/stack | solution.py:21
  98.7 14.4 %reshape.206 = bf16[2048,1536,1,1,1]{1,0,2,3,4:T(8,128)(2,1)} reshape(bf16[2,1024,3,2,256]{4,3,2,1,0:T(2,128)(2,1)} %pad_maximum_fusion) | data formatting | bytes 12582912 | tf_op jit(solution)/shard_map/reshape | solution.py:21
  118.2 4.9 %fusion.2 = f32[4,4,2,8,1536]{4,3,1,0,2:T(8,128)S(1)} fusion(bf16[2048,1536,1,1,1]{1,0,2,3,4:T(8,128)(2,1)} %reshape.206, bf16[4,4,2,8,2048]{4,3,2,1,0:T(8,128)(2,1)} %bitcast.64), kind=kOutput, calls=%fused_computation.6 | convolution fusion | flops 1610612736 | bytes 8912896 | tf_op jit(solution)/shard_map/dot_general | solution.py:63
  123.1 5.8 %all_to_all.45 = f32[4,4,2,8,1536]{4,3,1,0,2:T(8,128)} all-to-all(f32[4,4,2,8,1536]{4,3,1,0,2:T(8,128)S(1)} %fusion.2), channel_id=1, replica_groups=mesh['ylo'=2,'z'=8,'x'=4,'yhi'=4,'core'=2] {'core'}, dimensions={2} | all-to-all | bytes 3145728 | tf_op jit(solution)/shard_map/all_to_all | solution.py:31
  128.9 8.1 %all-to-all-start.5 = ((bf16[16,128,256]{2,1,0:T(8,128)(2,1)}), bf16[16,128,256]{2,1,0:T(8,128)(2,1)}, u32[]{:S(2)}, u32[]{:S(2)}) async-start(bf16[16,128,256]{2,1,0:T(8,128)(2,1)} %gather_fusion), calls=%async_computation.5 | async-start | bytes 2097152 | tf_op jit(solution)/shard_map/all_to_all | solution.py:53
  137.1 15.8 %maximum_bitcast_fusion.2 = (bf16[1,1024,3,2,256]{4,3,2,1,0:T(2,128)(2,1)S(1)}, bf16[1,1024,3,2,256]{4,3,2,1,0:T(2,128)(2,1)S(1)}) fusion(bf16[1024,3,1,256]{3,2,1,0:T(2,128)(2,1)} %get-tuple-element.18, bf16[1024,3,1,256]{3,2,1,0:T(2,128)(2,1)} %get-tuple-element.20, bf16[1024,3,1,256]{3,2,1,0:T(2,128)(2,1)S(1)} %get-tuple-element.19), kind=kLoop, calls=%fused_computation.10 | loop fusion | flops 12582912 | bytes 11010048 | tf_op jit(solution)/shard_map/stack | solution.py:21
  152.9 10.5 %pad_maximum_fusion.1 = bf16[2,1024,3,2,256]{4,3,2,1,0:T(2,128)(2,1)} fusion(bf16[1,1024,3,2,256]{4,3,2,1,0:T(2,128)(2,1)S(1)} %get-tuple-element.16, bf16[1,1024,3,2,256]{4,3,2,1,0:T(2,128)(2,1)S(1)} %get-tuple-element.15), kind=kLoop, calls=%fused_computation.3 | loop fusion | flops 3145728 | bytes 12582912 | tf_op jit(solution)/shard_map/stack | solution.py:21
  163.3 14.5 %reshape.207 = bf16[2048,1536,1,1,1]{1,0,2,3,4:T(8,128)(2,1)} reshape(bf16[2,1024,3,2,256]{4,3,2,1,0:T(2,128)(2,1)} %pad_maximum_fusion.1) | data formatting | bytes 12582912 | tf_op jit(solution)/shard_map/reshape | solution.py:21
  180.3 4.6 %fusion = f32[4,4,2,8,1536]{4,3,1,0,2:T(8,128)S(1)} fusion(bf16[2048,1536,1,1,1]{1,0,2,3,4:T(8,128)(2,1)} %reshape.207, bf16[4,4,2,8,2048]{4,3,2,1,0:T(8,128)(2,1)S(1)} %bitcast.65), kind=kOutput, calls=%fused_computation.4 | convolution fusion | flops 1610612736 | bytes 8912896 | tf_op jit(solution)/shard_map/dot_general | solution.py:63
  184.9 5.0 %all_to_all.46 = f32[4,4,2,8,1536]{4,3,1,0,2:T(8,128)S(1)} all-to-all(f32[4,4,2,8,1536]{4,3,1,0,2:T(8,128)S(1)} %fusion), channel_id=1, replica_groups=mesh['ylo'=2,'z'=8,'x'=4,'yhi'=4,'core'=2] {'core'}, dimensions={2} | all-to-all | bytes 3145728 | tf_op jit(solution)/shard_map/all_to_all | solution.py:31
  189.9 4.3 %all-to-all-start.3 = ((bf16[4,4,8,1536]{3,2,1,0:T(8,128)(2,1)}), bf16[4,4,8,1536]{3,2,1,0:T(8,128)(2,1)S(1)}, u32[]{:S(2)}, u32[]{:S(2)}) async-start(bf16[4,4,8,1536]{3,2,1,0:T(8,128)(2,1)} %reduce_sum.54), calls=%async_computation.3 | async-start | bytes 786432 | tf_op jit(solution)/shard_map/all_to_all | solution.py:33
  195.2 7.4 %all-to-all-done.3 = bf16[4,4,8,1536]{3,2,1,0:T(8,128)(2,1)S(1)} async-done(((bf16[4,4,8,1536]{3,2,1,0:T(8,128)(2,1)}), bf16[4,4,8,1536]{3,2,1,0:T(8,128)(2,1)S(1)}, u32[]{:S(2)}, u32[]{:S(2)}) %all-to-all-start.3) | async-done | bytes 393248 | tf_op jit(solution)/shard_map/all_to_all | solution.py:33
  202.6 3.5 %all-to-all-start.7 = ((bf16[4,4,8,1536]{3,2,1,0:T(8,128)(2,1)}), bf16[4,4,8,1536]{3,2,1,0:T(8,128)(2,1)S(1)}, u32[]{:S(2)}, u32[]{:S(2)}) async-start(bf16[4,4,8,1536]{3,2,1,0:T(8,128)(2,1)} %reduce_sum.57), calls=%async_computation.7 | async-start | bytes 786432 | tf_op jit(solution)/shard_map/all_to_all | solution.py:33
  206.8 6.6 %all-to-all-done.7 = bf16[4,4,8,1536]{3,2,1,0:T(8,128)(2,1)S(1)} async-done(((bf16[4,4,8,1536]{3,2,1,0:T(8,128)(2,1)}), bf16[4,4,8,1536]{3,2,1,0:T(8,128)(2,1)S(1)}, u32[]{:S(2)}, u32[]{:S(2)}) %all-to-all-start.7) | async-done | bytes 393248 | tf_op jit(solution)/shard_map/all_to_all | solution.py:33
  213.4 6.2 %all-to-all-start.4 = ((f32[4,8,1536]{2,1,0:T(8,128)}), f32[4,8,1536]{2,1,0:T(8,128)S(1)}, u32[]{:S(2)}, u32[]{:S(2)}) async-start(f32[4,8,1536]{2,1,0:T(8,128)} %convert_reduce_fusion.1), calls=%async_computation.4 | async-start | bytes 393216 | tf_op jit(solution)/shard_map/all_to_all | solution.py:35
  220.3 8.0 %all-to-all-done.4 = f32[4,8,1536]{2,1,0:T(8,128)S(1)} async-done(((f32[4,8,1536]{2,1,0:T(8,128)}), f32[4,8,1536]{2,1,0:T(8,128)S(1)}, u32[]{:S(2)}, u32[]{:S(2)}) %all-to-all-start.4) | async-done | bytes 196640 | tf_op jit(solution)/shard_map/all_to_all | solution.py:35
  228.3 3.4 %all-to-all-start.8 = ((f32[4,8,1536]{2,1,0:T(8,128)}), f32[4,8,1536]{2,1,0:T(8,128)S(1)}, u32[]{:S(2)}, u32[]{:S(2)}) async-start(f32[4,8,1536]{2,1,0:T(8,128)} %convert_reduce_fusion), calls=%async_computation.8 | async-start | bytes 393216 | tf_op jit(solution)/shard_map/all_to_all | solution.py:35
  231.8 8.6 %all-to-all-done.8 = f32[4,8,1536]{2,1,0:T(8,128)S(1)} async-done(((f32[4,8,1536]{2,1,0:T(8,128)}), f32[4,8,1536]{2,1,0:T(8,128)S(1)}, u32[]{:S(2)}, u32[]{:S(2)}) %all-to-all-start.8) | async-done | bytes 196640 | tf_op jit(solution)/shard_map/all_to_all | solution.py:35
  (47 shorter events, 15.0 us)
Async XLA Ops:
  0.0 13.3 %copy-start.7 = (bf16[2,3,2,1024]{3,2,1,0:T(2,128)(2,1)S(1)}, bf16[2,3,2,1024]{3,2,1,0:T(2,128)(2,1)}, u32[]{:S(2)}) copy-start(bf16[2,3,2,1024]{3,2,1,0:T(2,128)(2,1)} %param.4) | copy-start | bytes 73732
  0.0 61.2 %all-to-all-start = ((bf16[16,128,256]{2,1,0:T(8,128)(2,1)}), bf16[16,128,256]{2,1,0:T(8,128)(2,1)}, u32[]{:S(2)}, u32[]{:S(2)}) async-start(bf16[16,128,256]{2,1,0:T(8,128)(2,1)} %bitcast.63), calls=%async_computation | async-start | bytes 2097152 | tf_op jit(solution)/shard_map/all_to_all | solution.py:45
  13.3 20.6 %copy-start = (f32[1024,256]{1,0:T(8,128)}, f32[1024,256]{1,0:T(8,128)S(1)}, u32[]{:S(2)}) copy-start(f32[1024,256]{1,0:T(8,128)S(1)} %get-tuple-element.21) | copy-start | bytes 3145732
  13.3 20.6 %copy-start.1 = (f32[1024,256]{1,0:T(8,128)}, f32[1024,256]{1,0:T(8,128)S(1)}, u32[]{:S(2)}) copy-start(f32[1024,256]{1,0:T(8,128)S(1)} %get-tuple-element.22) | copy-start | bytes 3145732
  13.6 20.3 %copy-start.3 = (f32[1024,3]{1,0:T(8,128)}, f32[1024,3]{1,0:T(8,128)S(1)}, u32[]{:S(2)}) copy-start(f32[1024,3]{1,0:T(8,128)S(1)} %copy.19) | copy-start | bytes 36868
  13.9 20.1 %copy-start.4 = (f32[1024,3]{1,0:T(8,128)}, f32[1024,3]{1,0:T(8,128)S(1)}, u32[]{:S(2)}) copy-start(f32[1024,3]{1,0:T(8,128)S(1)} %copy.20) | copy-start | bytes 36868
  16.2 17.8 %copy-start.8 = (s32[2,16]{1,0:T(2,128)S(1)}, s32[2,16]{1,0:T(2,128)}, u32[]{:S(2)}) copy-start(s32[2,16]{1,0:T(2,128)} %param.5) | copy-start | bytes 388
  16.2 17.8 %copy-start.5 = (f32[1024,3]{1,0:T(8,128)S(1)}, f32[1024,3]{1,0:T(8,128)}, u32[]{:S(2)}) copy-start(f32[1024,3]{1,0:T(8,128)} %copy.23) | copy-start | bytes 36868
  16.2 17.8 %copy-start.6 = (f32[1024,3]{1,0:T(8,128)S(1)}, f32[1024,3]{1,0:T(8,128)}, u32[]{:S(2)}) copy-start(f32[1024,3]{1,0:T(8,128)} %copy.24) | copy-start | bytes 36868
  64.0 51.9 %all-to-all-start.1 = ((bf16[16,128,256]{2,1,0:T(8,128)(2,1)}), bf16[16,128,256]{2,1,0:T(8,128)(2,1)}, u32[]{:S(2)}, u32[]{:S(2)}) async-start(bf16[16,128,256]{2,1,0:T(8,128)(2,1)} %gather_fusion.1), calls=%async_computation.1 | async-start | bytes 2097152 | tf_op jit(solution)/shard_map/all_to_all | solution.py:53
  128.9 49.9 %all-to-all-start.5 = ((bf16[16,128,256]{2,1,0:T(8,128)(2,1)}), bf16[16,128,256]{2,1,0:T(8,128)(2,1)}, u32[]{:S(2)}, u32[]{:S(2)}) async-start(bf16[16,128,256]{2,1,0:T(8,128)(2,1)} %gather_fusion), calls=%async_computation.5 | async-start | bytes 2097152 | tf_op jit(solution)/shard_map/all_to_all | solution.py:53
  163.3 14.5 %copy-start.2 = (f32[4,4,2,8,1536]{4,3,1,0,2:T(8,128)S(1)}, f32[4,4,2,8,1536]{4,3,1,0,2:T(8,128)}, u32[]{:S(2)}) copy-start(f32[4,4,2,8,1536]{4,3,1,0,2:T(8,128)} %all_to_all.45) | copy-start | bytes 4718596
  189.9 12.7 %all-to-all-start.3 = ((bf16[4,4,8,1536]{3,2,1,0:T(8,128)(2,1)}), bf16[4,4,8,1536]{3,2,1,0:T(8,128)(2,1)S(1)}, u32[]{:S(2)}, u32[]{:S(2)}) async-start(bf16[4,4,8,1536]{3,2,1,0:T(8,128)(2,1)} %reduce_sum.54), calls=%async_computation.3 | async-start | bytes 786432 | tf_op jit(solution)/shard_map/all_to_all | solution.py:33
  202.6 10.8 %all-to-all-start.7 = ((bf16[4,4,8,1536]{3,2,1,0:T(8,128)(2,1)}), bf16[4,4,8,1536]{3,2,1,0:T(8,128)(2,1)S(1)}, u32[]{:S(2)}, u32[]{:S(2)}) async-start(bf16[4,4,8,1536]{3,2,1,0:T(8,128)(2,1)} %reduce_sum.57), calls=%async_computation.7 | async-start | bytes 786432 | tf_op jit(solution)/shard_map/all_to_all | solution.py:33
  213.4 14.9 %all-to-all-start.4 = ((f32[4,8,1536]{2,1,0:T(8,128)}), f32[4,8,1536]{2,1,0:T(8,128)S(1)}, u32[]{:S(2)}, u32[]{:S(2)}) async-start(f32[4,8,1536]{2,1,0:T(8,128)} %convert_reduce_fusion.1), calls=%async_computation.4 | async-start | bytes 393216 | tf_op jit(solution)/shard_map/all_to_all | solution.py:35
  228.3 12.1 %all-to-all-start.8 = ((f32[4,8,1536]{2,1,0:T(8,128)}), f32[4,8,1536]{2,1,0:T(8,128)S(1)}, u32[]{:S(2)}, u32[]{:S(2)}) async-start(f32[4,8,1536]{2,1,0:T(8,128)} %convert_reduce_fusion), calls=%async_computation.8 | async-start | bytes 393216 | tf_op jit(solution)/shard_map/all_to_all | solution.py:35

commit v2 on v1

v2 whole, which is shorter than its diff:
```python
import functools

import jax
import jax.numpy as jnp
from jax import lax
from jax.experimental import pallas as pl
from jax.experimental.pallas import tpu as pltpu
from jax.sharding import Mesh, PartitionSpec as P


KA = ("ylo", "z")
GRID = ("x", "yhi", "core")


def near(value):
    return pltpu.with_memory_space_constraint(value, pltpu.VMEM)


def weigh_kernel(fields_ref, own_ref, out_ref):
    num_q, _, _, width = out_ref.shape
    bands = own_ref.shape[-1]
    modes = width // (2 * bands)
    own_real = own_ref[0].astype(jnp.float32)
    own_imag = own_ref[1].astype(jnp.float32)
    for which in range(num_q):
        for mode in range(modes):
            at = 2 * (which * modes + mode)
            field_real = fields_ref[:, at : at + 1]
            field_imag = fields_ref[:, at + 1 : at + 2]
            part_real = (field_real * own_real - field_imag * own_imag).astype(jnp.bfloat16)
            part_imag = (field_real * own_imag + field_imag * own_real).astype(jnp.bfloat16)
            first = pl.ds(2 * mode * bands, bands)
            second = pl.ds((2 * mode + 1) * bands, bands)
            out_ref[which, 0, :, first] = part_real
            out_ref[which, 0, :, second] = part_imag
            out_ref[which, 1, :, first] = part_imag
            out_ref[which, 1, :, second] = -part_real


def weigh(fields, own, block=128):
    num_q, modes, _, rows = fields.shape
    bands = own.shape[-1]
    width = 2 * modes * bands
    columns = fields.reshape(num_q * modes * 2, rows).astype(jnp.float32).T
    out = pl.pallas_call(
        weigh_kernel,
        grid=(rows // block,),
        in_specs=[
            pl.BlockSpec((block, num_q * modes * 2), lambda i: (i, 0)),
            pl.BlockSpec((2, block, bands), lambda i: (0, i, 0)),
        ],
        out_specs=pl.BlockSpec((num_q, 2, block, width), lambda i: (0, 0, i, 0)),
        out_shape=jax.ShapeDtypeStruct((num_q, 2, rows, width), jnp.bfloat16),
        name="weigh",
    )(columns, own)
    return out.reshape(num_q, 2 * rows, width)


def couple_kernel(core_ref, fetched_ref, weighted_ref, keep_ref, send_ref, turned_ref, block_ref):
    @pl.when(pl.program_id(0) == 0)
    def _():
        turned_ref[...] = fetched_ref[...].T

    block_ref[...] = jnp.dot(turned_ref[...], weighted_ref[0], preferred_element_type=jnp.float32)
    pieces, rows, _ = keep_ref.shape
    cols = pl.ds(pl.multiple_of(pl.program_id(0) * block_ref.shape[1], 128), block_ref.shape[1])
    mine = core_ref[0] * rows
    other = rows - mine
    for piece in range(pieces):
        start = 2 * rows * piece
        keep_ref[piece, :, cols] = block_ref[pl.ds(pl.multiple_of(start + mine, 8), rows), :]
        send_ref[piece, :, cols] = block_ref[pl.ds(pl.multiple_of(start + other, 8), rows), :]


def couple(which, fetched, weighted, block=256):
    depth, bands = fetched.shape
    width = weighted.shape[-1]
    pieces = lax.axis_size("x") * lax.axis_size("yhi")
    rows = bands // (2 * pieces)
    half = pltpu.VMEM((pieces, rows, width), jnp.float32)
    return pl.pallas_call(
        couple_kernel,
        grid_spec=pltpu.PrefetchScalarGridSpec(
            num_scalar_prefetch=1,
            grid=(width // block,),
            in_specs=[
                pl.BlockSpec(memory_space=pltpu.VMEM),
                pl.BlockSpec((1, depth, block), lambda j, core: (which, 0, j)),
            ],
            out_specs=[pl.BlockSpec(memory_space=pltpu.VMEM)] * 2,
            scratch_shapes=[pltpu.VMEM((bands, depth), jnp.bfloat16), pltpu.VMEM((bands, block), jnp.float32)],
        ),
        out_shape=[half, half],
        name="couple",
    )(lax.axis_index("core").astype(jnp.int32).reshape(1), near(fetched), weighted)


def fold_kernel(x_ref, keep_ref, received_ref, *out_refs):
    count = len(out_refs)
    span = out_refs[0].shape[0]
    for shift, out_ref in enumerate(out_refs):
        start = lax.rem(x_ref[0] + shift, count) * span
        for piece in range(span):
            out_ref[piece] = (keep_ref[start + piece] + received_ref[start + piece]).astype(out_ref.dtype)


def fold(keep, received):
    xs = lax.axis_size("x")
    pieces, rows, width = keep.shape
    out = pltpu.VMEM((pieces // xs, rows, width), jnp.bfloat16)
    return pl.pallas_call(
        fold_kernel,
        grid_spec=pltpu.PrefetchScalarGridSpec(
            num_scalar_prefetch=1,
            grid=(),
            in_specs=[pl.BlockSpec(memory_space=pltpu.VMEM)] * 2,
            out_specs=[pl.BlockSpec(memory_space=pltpu.VMEM)] * xs,
        ),
        out_shape=[out] * xs,
        name="fold",
    )(lax.axis_index("x").astype(jnp.int32).reshape(1), near(keep), near(received))


def gather_x_kernel(counts, *refs):
    out_ref = refs[-1]
    start = 0
    for which, count in enumerate(counts):
        mine = refs[start : start + count]
        start += count
        for piece in range(out_ref.shape[0]):
            total = mine[0][piece].astype(jnp.float32)
            for ref in mine[1:]:
                total = total + ref[piece].astype(jnp.float32)
            out_ref[piece, which] = total


def gather_x(groups):
    span, rows, width = groups[0][0].shape
    flat = [part for group in groups for part in group]
    return pl.pallas_call(
        functools.partial(gather_x_kernel, tuple(len(group) for group in groups)),
        in_specs=[pl.BlockSpec(memory_space=pltpu.VMEM)] * len(flat),
        out_specs=pl.BlockSpec(memory_space=pltpu.VMEM),
        out_shape=pltpu.VMEM((span, len(groups), rows, width), jnp.float32),
        name="gather_x",
    )(*[near(part) for part in flat])


def final_kernel(parts_ref, out_ref):
    count, num_q, rows, _ = parts_ref.shape
    _, _, modes, _, _, bands = out_ref.shape
    for which in range(num_q):
        for col in range(2 * modes):
            cols = pl.ds(col * bands, bands)
            total = parts_ref[0, which, :, cols]
            for source in range(1, count):
                total = total + parts_ref[source, which, :, cols]
            for row in range(rows):
                out_ref[row, which, col // 2, col % 2] = total[row : row + 1]


def final(parts, modes):
    _, num_q, rows, width = parts.shape
    bands = width // (2 * modes)
    return pl.pallas_call(
        final_kernel,
        in_specs=[pl.BlockSpec(memory_space=pltpu.VMEM)],
        out_specs=pl.BlockSpec(memory_space=pltpu.VMEM),
        out_shape=jax.ShapeDtypeStruct((rows, num_q, modes, 2, 1, bands), jnp.float32),
        name="final",
    )(near(parts))


def pick_kernel(partner_ref, spread_ref, out_ref, sems):
    count = out_ref.shape[0]
    copies = [
        pltpu.make_async_copy(spread_ref.at[partner_ref[at]], out_ref.at[at], sems.at[at]) for at in range(count)
    ]
    for copy in copies:
        copy.start()
    for copy in copies:
        copy.wait()


def pick(spread, partner):
    return pl.pallas_call(
        pick_kernel,
        grid_spec=pltpu.PrefetchScalarGridSpec(
            num_scalar_prefetch=1,
            grid=(),
            in_specs=[pl.BlockSpec(memory_space=pltpu.VMEM)],
            out_specs=pl.BlockSpec(memory_space=pl.ANY),
            scratch_shapes=[pltpu.SemaphoreType.DMA((spread.shape[0],))],
        ),
        out_shape=jax.ShapeDtypeStruct(spread.shape, spread.dtype),
        name="pick",
    )(partner, near(spread))


def reduce_core_x(which, fetched, weighted):
    keep, send = couple(which, fetched, weighted)
    received = lax.ppermute(send, "core", [(0, 1), (1, 0)])
    parts = fold(keep, received)
    count = len(parts)
    moved = [
        lax.ppermute(parts[shift], "x", [(at, (at + shift) % count) for at in range(count)])
        for shift in range(1, count)
    ]
    return [parts[0], *moved]


def exchange(value, axis):
    return lax.all_to_all(value, axis, split_axis=0, concat_axis=0, tiled=True)


def per_device(orbitals, fields, partner):
    num_q, modes = fields.shape[:2]
    own = orbitals[0]
    rows, bands = own.shape[1:]
    points = lax.axis_size(KA)
    flat = own.reshape(points, 2 * rows // points, bands)
    spread = exchange(flat, KA)
    weighted = weigh(fields, own)
    picked = []
    for which in range(num_q):
        picked.append(pick(spread, partner[which]))
    fetched = []
    for which in range(num_q):
        if which:
            picked[which], fetched[-1] = lax.optimization_barrier((picked[which], fetched[-1]))
        fetched.append(exchange(picked[which], KA))
    groups = [reduce_core_x(which, fetched[which].reshape(2 * rows, bands), weighted) for which in range(num_q)]
    for which in range(num_q - 1):
        groups[which] = [gather_x([groups[which]])[:, 0]]
    parts = gather_x(groups)
    parts = exchange(parts, "yhi")
    return final(parts, modes)


def solution(mesh):
    fine = Mesh(mesh.devices.reshape(2, 8, 4, 4, 2), KA + GRID)

    return jax.shard_map(
        per_device,
        mesh=fine,
        in_specs=(P(KA, None, GRID, None), P(None, None, None, GRID), P()),
        out_specs=P(GRID, None, None, None, KA, None),
        check_vma=False,
    )
```

time: 243 us -> 165 us (0.68)
  the two profiles are of different devices: /device:TPU:8 before, /device:TPU:70 now
where the time goes in v2:
time: 165 us; the launch traced here: 164 us
  waiting for transfers between devices  63.9 us (39%)
  starting transfers between devices  44.1 us (27%)
  Pallas kernels  28.3 us (17%)
  blocking collectives  19.9 us (12%)
  local copies, waits for them, and re-layouts  7.16 us (4%)
    all_to_all x3, waiting for transfers between devices, exchange(): return lax.all_to_all(value, axis, split_axis=0, concat_axis=0, tiled=True)  59.2 us
    all_to_all x3, starting transfers between devices, exchange(): return lax.all_to_all(value, axis, split_axis=0, concat_axis=0, tiled=True)  21.3 us
    all_to_all x1, blocking collectives, exchange(): return lax.all_to_all(value, axis, split_axis=0, concat_axis=0, tiled=True)  19.9 us
    ppermute x6, starting transfers between devices, reduce_core_x(): lax.ppermute(parts[shift], 'x', [(at, (at + shift) % count) for at in ran...  19 us
    pallas_call x2, Pallas kernels, couple(): pl.pallas_call(couple_kernel, grid_spec=pltpu.PrefetchScalarGridSpec(num_...  14.3 us
    pallas_call x1, Pallas kernels, weigh(): pl.pallas_call(weigh_kernel, grid=(rows // block,), in_specs=[pl.BlockSpe...  8.3 us
    ppermute x6, waiting for transfers between devices, reduce_core_x(): lax.ppermute(parts[shift], 'x', [(at, (at + shift) % count) for at in ran...  4.75 us
    unnamed x8, local copies, waits for them, and re-layouts  4.06 us
  transfers between devices with their start and end apart: 11, of which 5 were waited for; matrix products, arithmetic and copies ran while one was open for 2% of the time, Pallas kernels for 16%

profile of v2, /device:TPU:70, one launch (start us, length us, event | category | flops | bytes accessed | tf_op | source)
XLA Modules:
  0.0 163.6 jit_solution(5425167218519283918)
XLA Ops:
  0.0 11.0 %all-to-all-start = ((bf16[16,128,256]{2,1,0:T(8,128)(2,1)}), bf16[16,128,256]{2,1,0:T(8,128)(2,1)S(1)}, u32[]{:S(2)}, u32[]{:S(2)}) async-start(bf16[16,128,256]{2,1,0:T(8,128)(2,1)} %bitcast.17), calls=%async_computation | async-start | bytes 2097152 | tf_op jit(solution)/shard_map/all_to_all | solution.py:213
  11.0 1.3 slice_bitcast_fusion
  12.3 26.1 %all-to-all-done.spread_ref = bf16[16,128,256]{2,1,0:T(8,128)(2,1)S(1)} async-done(((bf16[16,128,256]{2,1,0:T(8,128)(2,1)}), bf16[16,128,256]{2,1,0:T(8,128)(2,1)S(1)}, u32[]{:S(2)}, u32[]{:S(2)}) %all-to-all-start) | async-done | bytes 1048608 | tf_op jit(solution)/shard_map/all_to_all | solution.py:213
  38.5 1.8 %pick.3 = bf16[16,128,256]{2,1,0:T(8,128)(2,1)} custom-call(s32[16]{0:T(128)} %get-tuple-element.33.partner_ref, bf16[16,128,256]{2,1,0:T(8,128)(2,1)S(1)} %all-to-all-done.spread_ref), custom_call_target="tpu_custom_call" | custom-call | tf_op jit(solution)/shard_map/pick/pallas_call | solution.py:186
  40.3 4.9 %all-to-all-start.1 = ((bf16[16,128,256]{2,1,0:T(8,128)(2,1)}), bf16[16,128,256]{2,1,0:T(8,128)(2,1)S(1)}, u32[]{:S(2)}, u32[]{:S(2)}) async-start(bf16[16,128,256]{2,1,0:T(8,128)(2,1)} %pick.3), calls=%async_computation.1 | async-start | bytes 2097152 | tf_op jit(solution)/shard_map/all_to_all | solution.py:213
  45.2 1.8 %pick.2 = bf16[16,128,256]{2,1,0:T(8,128)(2,1)} custom-call(s32[16]{0:T(128)} %get-tuple-element.34.partner_ref, bf16[16,128,256]{2,1,0:T(8,128)(2,1)S(1)} %all-to-all-done.spread_ref), custom_call_target="tpu_custom_call" | custom-call | tf_op jit(solution)/shard_map/pick/pallas_call | solution.py:186
  47.1 25.5 %all-to-all-done.1 = bf16[16,128,256]{2,1,0:T(8,128)(2,1)S(1)} async-done(((bf16[16,128,256]{2,1,0:T(8,128)(2,1)}), bf16[16,128,256]{2,1,0:T(8,128)(2,1)S(1)}, u32[]{:S(2)}, u32[]{:S(2)}) %all-to-all-start.1) | async-done | bytes 1048608 | tf_op jit(solution)/shard_map/all_to_all | solution.py:213
  72.5 5.3 %all-to-all-start.2 = ((bf16[16,128,256]{2,1,0:T(8,128)(2,1)}), bf16[16,128,256]{2,1,0:T(8,128)(2,1)}, u32[]{:S(2)}, u32[]{:S(2)}) async-start(bf16[16,128,256]{2,1,0:T(8,128)(2,1)} %pick.2), calls=%async_computation.2 | async-start | bytes 2097152 | tf_op jit(solution)/shard_map/all_to_all | solution.py:213
  79.6 8.3 %weigh.1 = bf16[2,2,1024,1536]{3,2,1,0:T(8,128)(2,1)} custom-call(f32[1024,12]{1,0:T(8,128)} %bitcast.19, bf16[2,1024,256]{2,1,0:T(8,128)(2,1)} %bitcast.18), custom_call_target="tpu_custom_call" | custom-call | tf_op jit(solution)/shard_map/weigh/pallas_call | solution.py:45
  87.9 7.0 %couple.2 = (f32[16,8,1536]{2,1,0:T(8,128)S(1)}, f32[16,8,1536]{2,1,0:T(8,128)}) custom-call(s32[1]{0:T(128)} %bitcast.1.core_ref, bf16[2048,256]{1,0:T(8,128)(2,1)S(1)} %bitcast.13, bf16[2,2048,1536]{2,1,0:T(8,128)(2,1)} %bitcast.15), custom_call_target="tpu_custom_call" | custom-call | tf_op jit(solution)/shard_map/couple/pallas_call | solution.py:81
  95.8 1.9 %collective-permute-start = (f32[16,8,1536]{2,1,0:T(8,128)}, f32[16,8,1536]{2,1,0:T(8,128)S(1)}, u32[]{:S(2)}, u32[]{:S(2)}) collective-permute-start(f32[16,8,1536]{2,1,0:T(8,128)} %get-tuple-element.21), channel_id=1, source_target_pairs={{0,1},{1,0},{2,3},{3,2},{4,5},{5,4},{6,7},{7,6},{8,9},{9,8},{10,11... | collective-permute-start | bytes 2359304 | tf_op jit(solution)/shard_map/ppermute | solution.py:202
  97.7 7.6 %all-to-all-done.2 = bf16[16,128,256]{2,1,0:T(8,128)(2,1)} async-done(((bf16[16,128,256]{2,1,0:T(8,128)(2,1)}), bf16[16,128,256]{2,1,0:T(8,128)(2,1)}, u32[]{:S(2)}, u32[]{:S(2)}) %all-to-all-start.2) | async-done | bytes 1048608 | tf_op jit(solution)/shard_map/all_to_all | solution.py:213
  105.3 7.4 %couple.3 = (f32[16,8,1536]{2,1,0:T(8,128)S(1)}, f32[16,8,1536]{2,1,0:T(8,128)}) custom-call(s32[1]{0:T(128)} %bitcast.1.core_ref, bf16[2048,256]{1,0:T(8,128)(2,1)} %bitcast.10.fetched_ref, bf16[2,2048,1536]{2,1,0:T(8,128)(2,1)} %bitcast.16), custom_call_target="tpu_custom_call" | custom-call | tf_op jit(solution)/shard_map/couple/pallas_call | solution.py:81
  112.6 1.9 %collective-permute-start.4 = (f32[16,8,1536]{2,1,0:T(8,128)}, f32[16,8,1536]{2,1,0:T(8,128)}, u32[]{:S(2)}, u32[]{:S(2)}) collective-permute-start(f32[16,8,1536]{2,1,0:T(8,128)} %get-tuple-element.28), channel_id=1, source_target_pairs={{0,1},{1,0},{2,3},{3,2},{4,5},{5,4},{6,7},{7,6},{8,9},{9,8},{10,11... | collective-permute-start | bytes 2359304 | tf_op jit(solution)/shard_map/ppermute | solution.py:202
  117.8 2.4 %collective-permute-start.1 = (bf16[4,8,1536]{2,1,0:T(8,128)(2,1)S(1)}, bf16[4,8,1536]{2,1,0:T(8,128)(2,1)S(1)}, u32[]{:S(2)}, u32[]{:S(2)}) collective-permute-start(bf16[4,8,1536]{2,1,0:T(8,128)(2,1)S(1)} %get-tuple-element.23), channel_id=1, source_target_pairs={{0,8},{8,16},{16,24},{24,0},{1,9},{9,17},{17,25},{25,1},{2,10},{10... | collective-permute-start | bytes 294920 | tf_op jit(solution)/shard_map/ppermute | solution.py:206
  120.2 4.3 %collective-permute-start.2 = (bf16[4,8,1536]{2,1,0:T(8,128)(2,1)S(1)}, bf16[4,8,1536]{2,1,0:T(8,128)(2,1)S(1)}, u32[]{:S(2)}, u32[]{:S(2)}) collective-permute-start(bf16[4,8,1536]{2,1,0:T(8,128)(2,1)S(1)} %get-tuple-element.24), channel_id=1, source_target_pairs={{0,16},{8,24},{16,0},{24,8},{1,17},{9,25},{17,1},{25,9},{2,18},{10... | collective-permute-start | bytes 294920 | tf_op jit(solution)/shard_map/ppermute | solution.py:206
  124.5 1.9 %collective-permute-start.3 = (bf16[4,8,1536]{2,1,0:T(8,128)(2,1)S(1)}, bf16[4,8,1536]{2,1,0:T(8,128)(2,1)S(1)}, u32[]{:S(2)}, u32[]{:S(2)}) collective-permute-start(bf16[4,8,1536]{2,1,0:T(8,128)(2,1)S(1)} %get-tuple-element.25), channel_id=1, source_target_pairs={{0,24},{8,0},{16,8},{24,16},{1,25},{9,1},{17,9},{25,17},{2,26},{10... | collective-permute-start | bytes 294920 | tf_op jit(solution)/shard_map/ppermute | solution.py:206
  126.5 1.2 fold.3
  127.7 5.1 %collective-permute-start.5 = (bf16[4,8,1536]{2,1,0:T(8,128)(2,1)S(1)}, bf16[4,8,1536]{2,1,0:T(8,128)(2,1)S(1)}, u32[]{:S(2)}, u32[]{:S(2)}) collective-permute-start(bf16[4,8,1536]{2,1,0:T(8,128)(2,1)S(1)} %get-tuple-element.30), channel_id=1, source_target_pairs={{0,8},{8,16},{16,24},{24,0},{1,9},{9,17},{17,25},{25,1},{2,10},{10... | collective-permute-start | bytes 294920 | tf_op jit(solution)/shard_map/ppermute | solution.py:206
  132.8 1.9 %collective-permute-start.6 = (bf16[4,8,1536]{2,1,0:T(8,128)(2,1)S(1)}, bf16[4,8,1536]{2,1,0:T(8,128)(2,1)S(1)}, u32[]{:S(2)}, u32[]{:S(2)}) collective-permute-start(bf16[4,8,1536]{2,1,0:T(8,128)(2,1)S(1)} %get-tuple-element.31), channel_id=1, source_target_pairs={{0,16},{8,24},{16,0},{24,8},{1,17},{9,25},{17,1},{25,9},{2,18},{10... | collective-permute-start | bytes 294920 | tf_op jit(solution)/shard_map/ppermute | solution.py:206
  134.8 3.3 %collective-permute-start.7 = (bf16[4,8,1536]{2,1,0:T(8,128)(2,1)S(1)}, bf16[4,8,1536]{2,1,0:T(8,128)(2,1)S(1)}, u32[]{:S(2)}, u32[]{:S(2)}) collective-permute-start(bf16[4,8,1536]{2,1,0:T(8,128)(2,1)S(1)} %get-tuple-element.32), channel_id=1, source_target_pairs={{0,24},{8,0},{16,8},{24,16},{1,25},{9,1},{17,9},{25,17},{2,26},{10... | collective-permute-start | bytes 294920 | tf_op jit(solution)/shard_map/ppermute | solution.py:206
  138.2 3.3 %collective-permute-done.6.refs_3_ = bf16[4,8,1536]{2,1,0:T(8,128)(2,1)S(1)} collective-permute-done((bf16[4,8,1536]{2,1,0:T(8,128)(2,1)S(1)}, bf16[4,8,1536]{2,1,0:T(8,128)(2,1)S(1)}, u32[]{:S(2)}, u32[]{:S(2)}) %collective-permute-start.6) | collective-permute-done | bytes 98336 | tf_op jit(solution)/shard_map/ppermute | solution.py:206
  141.5 1.4 collective-permute-done.7.refs_4_
  143.0 19.9 %all_to_all.20.parts_ref = f32[4,2,8,1536]{3,2,1,0:T(8,128)S(1)} all-to-all(f32[4,2,8,1536]{3,2,1,0:T(8,128)S(1)} %gather_x.3), channel_id=1, replica_groups=mesh['ylo'=2,'z'=8,'x'=4,'yhi'=4,'core'=2] {'yhi'}, dimensions={0} | all-to-all | bytes 786432 | tf_op jit(solution)/shard_map/all_to_all | solution.py:213
  (20 shorter events, 6.7 us)
Async XLA Ops:
  0.0 38.5 %all-to-all-start = ((bf16[16,128,256]{2,1,0:T(8,128)(2,1)}), bf16[16,128,256]{2,1,0:T(8,128)(2,1)S(1)}, u32[]{:S(2)}, u32[]{:S(2)}) async-start(bf16[16,128,256]{2,1,0:T(8,128)(2,1)} %bitcast.17), calls=%async_computation | async-start | bytes 2097152 | tf_op jit(solution)/shard_map/all_to_all | solution.py:213
  40.3 32.3 %all-to-all-start.1 = ((bf16[16,128,256]{2,1,0:T(8,128)(2,1)}), bf16[16,128,256]{2,1,0:T(8,128)(2,1)S(1)}, u32[]{:S(2)}, u32[]{:S(2)}) async-start(bf16[16,128,256]{2,1,0:T(8,128)(2,1)} %pick.3), calls=%async_computation.1 | async-start | bytes 2097152 | tf_op jit(solution)/shard_map/all_to_all | solution.py:213
  72.5 32.8 %all-to-all-start.2 = ((bf16[16,128,256]{2,1,0:T(8,128)(2,1)}), bf16[16,128,256]{2,1,0:T(8,128)(2,1)}, u32[]{:S(2)}, u32[]{:S(2)}) async-start(bf16[16,128,256]{2,1,0:T(8,128)(2,1)} %pick.2), calls=%async_computation.2 | async-start | bytes 2097152 | tf_op jit(solution)/shard_map/all_to_all | solution.py:213
  94.9 0.9 copy-start
  95.8 18.8 %collective-permute-start = (f32[16,8,1536]{2,1,0:T(8,128)}, f32[16,8,1536]{2,1,0:T(8,128)S(1)}, u32[]{:S(2)}, u32[]{:S(2)}) collective-permute-start(f32[16,8,1536]{2,1,0:T(8,128)} %get-tuple-element.21), channel_id=1, source_target_pairs={{0,1},{1,0},{2,3},{3,2},{4,5},{5,4},{6,7},{7,6},{8,9},{9,8},{10,11... | collective-permute-start | bytes 2359304 | tf_op jit(solution)/shard_map/ppermute | solution.py:202
  112.6 13.8 %collective-permute-start.4 = (f32[16,8,1536]{2,1,0:T(8,128)}, f32[16,8,1536]{2,1,0:T(8,128)}, u32[]{:S(2)}, u32[]{:S(2)}) collective-permute-start(f32[16,8,1536]{2,1,0:T(8,128)} %get-tuple-element.28), channel_id=1, source_target_pairs={{0,1},{1,0},{2,3},{3,2},{4,5},{5,4},{6,7},{7,6},{8,9},{9,8},{10,11... | collective-permute-start | bytes 2359304 | tf_op jit(solution)/shard_map/ppermute | solution.py:202
  114.6 0.9 copy-start.2
  115.5 1.1 copy-start.1
  116.6 1.1 copy-start.3
  117.8 17.0 %collective-permute-start.1 = (bf16[4,8,1536]{2,1,0:T(8,128)(2,1)S(1)}, bf16[4,8,1536]{2,1,0:T(8,128)(2,1)S(1)}, u32[]{:S(2)}, u32[]{:S(2)}) collective-permute-start(bf16[4,8,1536]{2,1,0:T(8,128)(2,1)S(1)} %get-tuple-element.23), channel_id=1, source_target_pairs={{0,8},{8,16},{16,24},{24,0},{1,9},{9,17},{17,25},{25,1},{2,10},{10... | collective-permute-start | bytes 294920 | tf_op jit(solution)/shard_map/ppermute | solution.py:206
  120.2 17.9 %collective-permute-start.2 = (bf16[4,8,1536]{2,1,0:T(8,128)(2,1)S(1)}, bf16[4,8,1536]{2,1,0:T(8,128)(2,1)S(1)}, u32[]{:S(2)}, u32[]{:S(2)}) collective-permute-start(bf16[4,8,1536]{2,1,0:T(8,128)(2,1)S(1)} %get-tuple-element.24), channel_id=1, source_target_pairs={{0,16},{8,24},{16,0},{24,8},{1,17},{9,25},{17,1},{25,9},{2,18},{10... | collective-permute-start | bytes 294920 | tf_op jit(solution)/shard_map/ppermute | solution.py:206
  124.5 13.6 %collective-permute-start.3 = (bf16[4,8,1536]{2,1,0:T(8,128)(2,1)S(1)}, bf16[4,8,1536]{2,1,0:T(8,128)(2,1)S(1)}, u32[]{:S(2)}, u32[]{:S(2)}) collective-permute-start(bf16[4,8,1536]{2,1,0:T(8,128)(2,1)S(1)} %get-tuple-element.25), channel_id=1, source_target_pairs={{0,24},{8,0},{16,8},{24,16},{1,25},{9,1},{17,9},{25,17},{2,26},{10... | collective-permute-start | bytes 294920 | tf_op jit(solution)/shard_map/ppermute | solution.py:206
  127.7 10.5 %collective-permute-start.5 = (bf16[4,8,1536]{2,1,0:T(8,128)(2,1)S(1)}, bf16[4,8,1536]{2,1,0:T(8,128)(2,1)S(1)}, u32[]{:S(2)}, u32[]{:S(2)}) collective-permute-start(bf16[4,8,1536]{2,1,0:T(8,128)(2,1)S(1)} %get-tuple-element.30), channel_id=1, source_target_pairs={{0,8},{8,16},{16,24},{24,0},{1,9},{9,17},{17,25},{25,1},{2,10},{10... | collective-permute-start | bytes 294920 | tf_op jit(solution)/shard_map/ppermute | solution.py:206
  132.8 8.7 %collective-permute-start.6 = (bf16[4,8,1536]{2,1,0:T(8,128)(2,1)S(1)}, bf16[4,8,1536]{2,1,0:T(8,128)(2,1)S(1)}, u32[]{:S(2)}, u32[]{:S(2)}) collective-permute-start(bf16[4,8,1536]{2,1,0:T(8,128)(2,1)S(1)} %get-tuple-element.31), channel_id=1, source_target_pairs={{0,16},{8,24},{16,0},{24,8},{1,17},{9,25},{17,1},{25,9},{2,18},{10... | collective-permute-start | bytes 294920 | tf_op jit(solution)/shard_map/ppermute | solution.py:206
  134.8 8.2 %collective-permute-start.7 = (bf16[4,8,1536]{2,1,0:T(8,128)(2,1)S(1)}, bf16[4,8,1536]{2,1,0:T(8,128)(2,1)S(1)}, u32[]{:S(2)}, u32[]{:S(2)}) collective-permute-start(bf16[4,8,1536]{2,1,0:T(8,128)(2,1)S(1)} %get-tuple-element.32), channel_id=1, source_target_pairs={{0,24},{8,0},{16,8},{24,16},{1,25},{9,1},{17,9},{25,17},{2,26},{10... | collective-permute-start | bytes 294920 | tf_op jit(solution)/shard_map/ppermute | solution.py:206

commit v3 on v1

v3 whole, which is shorter than its diff:
```python
import jax
import jax.numpy as jnp
from jax import lax
from jax.experimental import pallas as pl
from jax.experimental.pallas import tpu as pltpu
from jax.sharding import Mesh, PartitionSpec as P


KA = ("ylo", "z")
GRID = ("x", "yhi", "core")
WHOLE = pl.BlockSpec(memory_space=pltpu.VMEM)
PARAMS = pltpu.CompilerParams(vmem_limit_bytes=16 << 20)


def far(value):
    return pltpu.with_memory_space_constraint(value, pltpu.HBM)


def near(value):
    return pltpu.with_memory_space_constraint(value, pltpu.VMEM)


def weigh_kernel(fields_ref, own_ref, out_ref):
    bands = own_ref.shape[-1]
    own_real = own_ref[0].astype(jnp.float32)
    own_imag = own_ref[1].astype(jnp.float32)
    for mode in range(out_ref.shape[-1] // bands):
        field_real = fields_ref[:, 2 * mode : 2 * mode + 1]
        field_imag = fields_ref[:, 2 * mode + 1 : 2 * mode + 2]
        cols = slice(mode * bands, (mode + 1) * bands)
        out_ref[0, :, cols] = (field_real * own_real - field_imag * own_imag).astype(jnp.bfloat16)
        out_ref[1, :, cols] = (field_real * own_imag + field_imag * own_real).astype(jnp.bfloat16)


def weigh(field, own, block=256):
    modes, _, rows = field.shape
    bands = own.shape[-1]
    columns = field.reshape(modes * 2, rows).astype(jnp.float32).T
    out = pl.pallas_call(
        weigh_kernel,
        grid=(rows // block,),
        in_specs=[
            pl.BlockSpec((block, modes * 2), lambda i: (i, 0)),
            pl.BlockSpec((2, block, bands), lambda i: (0, i, 0)),
        ],
        out_specs=pl.BlockSpec((2, block, modes * bands), lambda i: (0, i, 0)),
        out_shape=pltpu.HBM((2, rows, modes * bands), jnp.bfloat16),
        compiler_params=PARAMS,
        name="weigh",
    )(columns, own)
    return out.reshape(2 * rows, modes * bands)


def pick_kernel(partner_ref, spread_ref, out_ref):
    for which in range(out_ref.shape[0]):
        for at in range(out_ref.shape[1]):
            out_ref[which, at] = spread_ref[partner_ref[which, at]]


def pick(spread, partner):
    return pl.pallas_call(
        pick_kernel,
        grid_spec=pltpu.PrefetchScalarGridSpec(num_scalar_prefetch=1, grid=(), in_specs=[WHOLE], out_specs=WHOLE),
        out_shape=pltpu.VMEM(partner.shape + spread.shape[1:], spread.dtype),
        compiler_params=PARAMS,
        name="pick",
    )(partner, near(spread))


def turn(fetched_ref, left_ref):
    bands = fetched_ref.shape[1]
    rows = fetched_ref.shape[0] // 2
    turned = fetched_ref[...].T
    left_ref[:bands] = turned
    left_ref[bands:, :rows] = -turned[:, rows:]
    left_ref[bands:, rows:] = turned[:, :rows]


def couple_kernel(core_ref, fetched_ref, own_ref, other_hbm, out_ref, left_ref, sum_ref, other_ref, sem):
    copy = pltpu.make_async_copy(other_hbm, other_ref, sem)
    copy.start()
    pieces, rows, width = out_ref.shape
    bands = pieces * rows
    turn(fetched_ref.at[core_ref[0]], left_ref.at[0])
    turn(fetched_ref.at[1 - core_ref[0]], left_ref.at[1])
    for start in range(0, width // 2, bands):
        cols = slice(start, start + bands)
        sum_ref[:, cols] = jnp.dot(left_ref[0], own_ref[:, cols], preferred_element_type=jnp.float32)
    copy.wait()
    for start in range(0, width // 2, bands):
        cols = slice(start, start + bands)
        total = sum_ref[:, cols] + jnp.dot(left_ref[1], other_ref[:, cols], preferred_element_type=jnp.float32)
        total = total.astype(out_ref.dtype).reshape(2, pieces, rows, bands)
        for part in range(2):
            at = 2 * start + part * bands
            out_ref[:, :, at : at + bands] = total[part]


def couple(core, fetched, own, other):
    _, depth, bands = fetched.shape
    width = own.shape[-1]
    pieces = lax.axis_size(GRID)
    return pl.pallas_call(
        couple_kernel,
        grid_spec=pltpu.PrefetchScalarGridSpec(
            num_scalar_prefetch=1,
            grid=(),
            in_specs=[WHOLE, WHOLE, pl.BlockSpec(memory_space=pltpu.HBM)],
            out_specs=WHOLE,
            scratch_shapes=[
                pltpu.VMEM((2, 2 * bands, depth), jnp.bfloat16),
                pltpu.VMEM((2 * bands, width), jnp.float32),
                pltpu.VMEM(other.shape, other.dtype),
                pltpu.SemaphoreType.DMA(()),
            ],
        ),
        out_shape=pltpu.VMEM((pieces, bands // pieces, 2 * width), jnp.bfloat16),
        compiler_params=PARAMS,
        name="couple",
    )(core.astype(jnp.int32).reshape(1), near(fetched), near(own), far(other))


def final_kernel(parts_ref, out_ref):
    rows, num_q, modes, _, _, bands = out_ref.shape
    for which in range(num_q):
        for col in range(2 * modes):
            cols = slice(col * bands, (col + 1) * bands)
            total = parts_ref[which, :, cols].astype(jnp.float32)
            for source in range(which + num_q, parts_ref.shape[0], num_q):
                total = total + parts_ref[source, :, cols].astype(jnp.float32)
            for row in range(rows):
                out_ref[row, which, col // 2, col % 2] = total[row : row + 1]


def final(parts, num_q, modes):
    _, rows, width = parts.shape
    return pl.pallas_call(
        final_kernel,
        in_specs=[WHOLE],
        out_specs=WHOLE,
        out_shape=jax.ShapeDtypeStruct((rows, num_q, modes, 2, 1, width // (2 * modes)), jnp.float32),
        compiler_params=PARAMS,
        name="final",
    )(near(parts))


def exchange(value, axis):
    return lax.all_to_all(value, axis, split_axis=0, concat_axis=0, tiled=True)


def swap(value):
    return lax.ppermute(value, "core", [(0, 1), (1, 0)])


def per_device(orbitals, fields, partner):
    num_q, modes = fields.shape[:2]
    own = orbitals[0]
    rows, bands = own.shape[1:]
    points = lax.axis_size(KA)
    depth = 2 * rows // points
    core = lax.axis_index("core")
    spread = exchange(own.reshape(points, depth, bands), KA)
    other = swap(own)
    other_field = swap(lax.dynamic_index_in_dim(fields, 1 - core, 0, keepdims=False))
    field = lax.dynamic_index_in_dim(fields, core, 0, keepdims=False)
    own_weighted = weigh(field, own)
    other_weighted = weigh(other_field, other)
    picked = pick(spread, partner)
    fetched = exchange(picked.reshape(num_q * points, depth, bands), ("core",) + KA)
    product = couple(core, fetched.reshape(2, 2 * rows, bands), own_weighted, other_weighted)
    parts = exchange(product, GRID)
    return final(parts, num_q, modes)


def solution(mesh):
    fine = Mesh(mesh.devices.reshape(2, 8, 4, 4, 2), KA + GRID)

    return jax.shard_map(
        per_device,
        mesh=fine,
        in_specs=(P(KA, None, GRID, None), P(None, None, None, GRID), P()),
        out_specs=P(GRID, None, None, None, KA, None),
        check_vma=False,
    )
```

time: 243 us -> 141 us (0.58)
  other arithmetic: 103 us -> 0.03 us
  blocking collectives: 10.8 us -> 70.5 us
  local copies, waits for them, and re-layouts: 41.3 us -> 3.09 us
  starting transfers between devices: 45.5 us -> 10.4 us
  Pallas kernels: 0 us -> 19.5 us
  matrix products: 9.49 us -> 0 us
  waiting for transfers between devices: 30.7 us -> 36.8 us
    all_to_all x2, blocking collectives: 10.8 us -> 70.5 us  [exchange(): return lax.all_to_all(value, axis, split_axis=0, concat_axis=0, tiled=True)]
    another operation x5 -> x0, other arithmetic: 53.5 us -> none  [the longest x4 52.8 us: weigh(): return jnp.stack([upper, lower], axis=0).reshape(2 * rows, -1)]
    all_to_all x7 -> x1, starting transfers between devices: 45.5 us -> 6.04 us  [exchange(): return lax.all_to_all(value, axis, split_axis=0, concat_axis=0, tiled=True)]
    reshape x4 -> x0, local copies, waits for them, and re-layouts: 32.7 us -> none  [the longest x2 29 us: weigh(): return jnp.stack([upper, lower], axis=0).reshape(2 * rows, -1)]
    neg x1 -> x0, other arithmetic: 27.1 us -> none  [weigh(): lower = jnp.stack([part_imag, -part_real], axis=2)]
    pallas_call x0 -> x5, Pallas kernels: none -> 19.5 us  [the longest x2 8.78 us: weigh(): pl.pallas_call(weigh_kernel, grid=(rows // block,), in_specs=[pl.BlockSpe...]
    convert_element_type x2 -> x0, other arithmetic: 19.1 us -> none  [the longest x1 17.7 us: weigh(): (field_real * own_imag + field_imag * own_real).astype(jnp.bfloat16)]
    dot_general x2 -> x0, matrix products: 9.49 us -> none  [finish(): lax.dot_general(lhs, weighted, (((0,), (0,)), ((), ())), preferred_elemen...]
  transfers between devices with their start and end apart: 7 -> 3, of which waited for: 4 -> 1; matrix products, arithmetic and copies ran while one was open for 57% -> 1% of each run, Pallas kernels for 0% -> 6%
where the time goes in v3:
time: 141 us; the launch traced here: 140 us
  blocking collectives  70.5 us (50%)
  waiting for transfers between devices  36.8 us (26%)
  Pallas kernels  19.5 us (14%)
  starting transfers between devices  10.4 us (7%)
  local copies, waits for them, and re-layouts  3.09 us (2%)
    all_to_all x2, blocking collectives, exchange(): return lax.all_to_all(value, axis, split_axis=0, concat_axis=0, tiled=True)  70.5 us
    all_to_all x1, waiting for transfers between devices, exchange(): return lax.all_to_all(value, axis, split_axis=0, concat_axis=0, tiled=True)  36.8 us
    pallas_call x2, Pallas kernels, weigh(): pl.pallas_call(weigh_kernel, grid=(rows // block,), in_specs=[pl.BlockSpe...  8.78 us
    pallas_call x1, Pallas kernels, couple(): pl.pallas_call(couple_kernel, grid_spec=pltpu.PrefetchScalarGridSpec(num_...  7.92 us
    all_to_all x1, starting transfers between devices, exchange(): return lax.all_to_all(value, axis, split_axis=0, concat_axis=0, tiled=True)  6.04 us
    ppermute x2, starting transfers between devices, swap(): return lax.ppermute(value, 'core', [(0, 1), (1, 0)])  4.33 us
  transfers between devices with their start and end apart: 3, of which 1 were waited for; matrix products, arithmetic and copies ran while one was open for 1% of the time, Pallas kernels for 6%

profile of v3, /device:TPU:8, one launch (start us, length us, event | category | flops | bytes accessed | tf_op | source)
XLA Modules:
  0.0 140.4 jit_solution(12628250836794417963)
XLA Ops:
  0.0 37.9 %all_to_all.15.spread_ref = bf16[16,128,256]{2,1,0:T(8,128)(2,1)S(1)} all-to-all(bf16[16,128,256]{2,1,0:T(8,128)(2,1)} %bitcast.1), channel_id=1, replica_groups=mesh['ylo'=2,'z'=8,'x'=4,'yhi'=4,'core'=2] {'ylo','z'}, dimensions={0} | all-to-all | bytes 2097152 | tf_op jit(solution)/shard_map/all_to_all | solution.py:148
  37.9 0.0 copy-start.2
  37.9 0.7 copy-done.2
  38.6 0.0 copy-start.3
  38.6 2.1 %pick.1 = bf16[2,16,128,256]{3,2,1,0:T(8,128)(2,1)} custom-call(s32[2,16]{1,0:T(2,128)S(1)} %copy-done.2, bf16[16,128,256]{2,1,0:T(8,128)(2,1)S(1)} %all_to_all.15.spread_ref), custom_call_target="tpu_custom_call" | custom-call | tf_op jit(solution)/shard_map/pick/pallas_call | solution.py:61
  40.7 6.0 %all-to-all-start.1 = ((bf16[32,128,256]{2,1,0:T(8,128)(2,1)}), bf16[32,128,256]{2,1,0:T(8,128)(2,1)}, u32[]{:S(2)}, u32[]{:S(2)}) async-start(bf16[32,128,256]{2,1,0:T(8,128)(2,1)} %bitcast.2), calls=%async_computation.1 | async-start | bytes 4194304 | tf_op jit(solution)/shard_map/all_to_all | solution.py:148
  46.7 2.1 %collective-permute-start.1 = (bf16[2,1024,256]{2,1,0:T(8,128)(2,1)}, bf16[2,1024,256]{2,1,0:T(8,128)(2,1)}, u32[]{:S(2)}, u32[]{:S(2)}) collective-permute-start(bf16[2,1024,256]{2,1,0:T(8,128)(2,1)} %bitcast.5.own_ref), channel_id=1, source_target_pairs={{0,1},{1,0},{2,3},{3,2},{4,5},{5,4},{6,7},{7,6},{8,9},{9,8},{10,11... | collective-permute-start | bytes 3145736 | tf_op jit(solution)/shard_map/ppermute | solution.py:152
  48.8 0.0 copy-done.3
  48.8 2.3 %collective-permute-start = (bf16[3,2,1024]{2,1,0:T(2,128)(2,1)S(1)}, bf16[3,2,1024]{2,1,0:T(2,128)(2,1)S(1)}, u32[]{:S(2)}, u32[]{:S(2)}) collective-permute-start(bf16[3,2,1024]{2,1,0:T(2,128)(2,1)S(1)} %get-tuple-element.5), channel_id=1, source_target_pairs={{0,1},{1,0},{2,3},{3,2},{4,5},{5,4},{6,7},{7,6},{8,9},{9,8},{10,11... | collective-permute-start | bytes 36872 | tf_op jit(solution)/shard_map/ppermute | solution.py:152
  51.1 0.2 copy.5
  51.4 4.4 %weigh.2 = bf16[2,1024,768]{2,1,0:T(8,128)(2,1)} custom-call(f32[1024,6]{1,0:T(8,128)S(1)} %bitcast.13, bf16[2,1024,256]{2,1,0:T(8,128)(2,1)} %bitcast.5.own_ref), custom_call_target="tpu_custom_call" | custom-call | tf_op jit(solution)/shard_map/weigh/pallas_call | solution.py:39
  55.8 0.0 copy-start
  55.8 0.0 collective-permute-done
  55.8 1.0 copy.6
  56.8 0.0 collective-permute-done.1.own_ref
  56.8 0.0 copy-start.1
  56.8 1.1 copy-done.1
  57.9 4.4 %weigh.3 = bf16[2,1024,768]{2,1,0:T(8,128)(2,1)} custom-call(f32[1024,6]{1,0:T(8,128)S(1)} %bitcast.12, bf16[2,1024,256]{2,1,0:T(8,128)(2,1)} %collective-permute-done.1.own_ref), custom_call_target="tpu_custom_call" | custom-call | tf_op jit(solution)/shard_map/weigh/pallas_call | solution.py:39
  62.3 36.8 %all-to-all-done.1 = bf16[32,128,256]{2,1,0:T(8,128)(2,1)} async-done(((bf16[32,128,256]{2,1,0:T(8,128)(2,1)}), bf16[32,128,256]{2,1,0:T(8,128)(2,1)}, u32[]{:S(2)}, u32[]{:S(2)}) %all-to-all-start.1) | async-done | bytes 2097184 | tf_op jit(solution)/shard_map/all_to_all | solution.py:148
  99.1 0.0 copy-done
  99.1 7.9 %couple.1 = bf16[32,8,1536]{2,1,0:T(8,128)(2,1)S(1)} custom-call(s32[1]{0:T(128)} %bitcast.core_ref, bf16[2,2048,256]{2,1,0:T(8,128)(2,1)} %bitcast.3.fetched_ref, bf16[2048,768]{1,0:T(8,128)(2,1)S(1)} %bitcast.11, bf16[2048,768]{1,0:T(8,128)(2,1)} %bitcast.14), custom_call_target="tpu_custom_call" | custom-call | tf_op jit(solution)/shard_map/couple/pallas_call | solution.py:103
  107.1 32.6 %all_to_all.16.parts_ref = bf16[32,8,1536]{2,1,0:T(8,128)(2,1)S(1)} all-to-all(bf16[32,8,1536]{2,1,0:T(8,128)(2,1)S(1)} %couple.1), channel_id=1, replica_groups=mesh['ylo'=2,'z'=8,'x'=4,'yhi'=4,'core'=2] {'x','yhi','core'}, dimensions={0} | all-to-all | bytes 1572864 | tf_op jit(solution)/shard_map/all_to_all | solution.py:148
  139.6 0.8 final.1
  (3 shorter events, 0.1 us)
Async XLA Ops:
  37.9 0.7 copy-start.2
  38.6 10.2 %copy-start.3 = (bf16[2,3,2,1024]{3,2,1,0:T(2,128)(2,1)S(1)}, bf16[2,3,2,1024]{3,2,1,0:T(2,128)(2,1)}, u32[]{:S(2)}) copy-start(bf16[2,3,2,1024]{3,2,1,0:T(2,128)(2,1)} %param.4) | copy-start | bytes 73732
  40.7 58.5 %all-to-all-start.1 = ((bf16[32,128,256]{2,1,0:T(8,128)(2,1)}), bf16[32,128,256]{2,1,0:T(8,128)(2,1)}, u32[]{:S(2)}, u32[]{:S(2)}) async-start(bf16[32,128,256]{2,1,0:T(8,128)(2,1)} %bitcast.2), calls=%async_computation.1 | async-start | bytes 4194304 | tf_op jit(solution)/shard_map/all_to_all | solution.py:148
  46.7 10.1 %collective-permute-start.1 = (bf16[2,1024,256]{2,1,0:T(8,128)(2,1)}, bf16[2,1024,256]{2,1,0:T(8,128)(2,1)}, u32[]{:S(2)}, u32[]{:S(2)}) collective-permute-start(bf16[2,1024,256]{2,1,0:T(8,128)(2,1)} %bitcast.5.own_ref), channel_id=1, source_target_pairs={{0,1},{1,0},{2,3},{3,2},{4,5},{5,4},{6,7},{7,6},{8,9},{9,8},{10,11... | collective-permute-start | bytes 3145736 | tf_op jit(solution)/shard_map/ppermute | solution.py:152
  48.8 6.9 %collective-permute-start = (bf16[3,2,1024]{2,1,0:T(2,128)(2,1)S(1)}, bf16[3,2,1024]{2,1,0:T(2,128)(2,1)S(1)}, u32[]{:S(2)}, u32[]{:S(2)}) collective-permute-start(bf16[3,2,1024]{2,1,0:T(2,128)(2,1)S(1)} %get-tuple-element.5), channel_id=1, source_target_pairs={{0,1},{1,0},{2,3},{3,2},{4,5},{5,4},{6,7},{7,6},{8,9},{9,8},{10,11... | collective-permute-start | bytes 36872 | tf_op jit(solution)/shard_map/ppermute | solution.py:152
  55.8 43.4 %copy-start = (bf16[2,1024,768]{2,1,0:T(8,128)(2,1)S(1)}, bf16[2,1024,768]{2,1,0:T(8,128)(2,1)}, u32[]{:S(2)}) copy-start(bf16[2,1024,768]{2,1,0:T(8,128)(2,1)} %weigh.2) | copy-start | bytes 9437188
  56.8 1.1 copy-start.1

commit v4 on v3

v4 whole, which is shorter than its diff:
```python
import jax
import jax.numpy as jnp
from jax import lax
from jax.experimental import pallas as pl
from jax.experimental.pallas import tpu as pltpu
from jax.sharding import Mesh, PartitionSpec as P


KA = ("ylo", "z")
GRID = ("xhi", "xlo", "yhi", "core")
TEAM = ("xlo", "core")
REDUCE = ("xhi", "yhi", "core")
WHOLE = pl.BlockSpec(memory_space=pltpu.VMEM)
PARAMS = pltpu.CompilerParams(vmem_limit_bytes=24 << 20)


def far(value):
    return pltpu.with_memory_space_constraint(value, pltpu.HBM)


def near(value):
    return pltpu.with_memory_space_constraint(value, pltpu.VMEM)


def weigh_kernel(fields_ref, own_ref, out_ref):
    bands = own_ref.shape[-1]
    own_real = own_ref[0].astype(jnp.float32)
    own_imag = own_ref[1].astype(jnp.float32)
    for mode in range(out_ref.shape[-1] // bands):
        field_real = fields_ref[:, 2 * mode : 2 * mode + 1]
        field_imag = fields_ref[:, 2 * mode + 1 : 2 * mode + 2]
        cols = slice(mode * bands, (mode + 1) * bands)
        out_ref[0, :, cols] = (field_real * own_real - field_imag * own_imag).astype(jnp.bfloat16)
        out_ref[1, :, cols] = (field_real * own_imag + field_imag * own_real).astype(jnp.bfloat16)


def weigh(field, own, block=256):
    modes, _, rows = field.shape
    bands = own.shape[-1]
    columns = field.reshape(modes * 2, rows).astype(jnp.float32).T
    out = pl.pallas_call(
        weigh_kernel,
        grid=(rows // block,),
        in_specs=[
            pl.BlockSpec((block, modes * 2), lambda i: (i, 0)),
            pl.BlockSpec((2, block, bands), lambda i: (0, i, 0)),
        ],
        out_specs=pl.BlockSpec((2, block, modes * bands), lambda i: (0, i, 0)),
        out_shape=pltpu.HBM((2, rows, modes * bands), jnp.bfloat16),
        compiler_params=PARAMS,
        name="weigh",
    )(columns, own)
    return out.reshape(2 * rows, modes * bands)


def pick_kernel(partner_ref, spread_ref, out_hbm, out_ref, sems):
    num_q, points = out_ref.shape[1:3]
    lanes = out_ref.shape[-1]
    quarter = lanes // 2
    step = points // 4
    low = lax.broadcasted_iota(jnp.int32, out_ref.shape[3:], 1) < quarter
    copies = []
    for which in range(num_q):
        for at in range(points):
            block = spread_ref[partner_ref[which, at]].astype(jnp.float32)
            left, right = block[:, :lanes], block[:, lanes:]
            even = jnp.where(low, left, pltpu.roll(right, quarter, 1))
            odd = jnp.where(low, pltpu.roll(left, quarter, 1), right)
            out_ref[0, which, at] = even.astype(out_ref.dtype)
            out_ref[1, which, at] = odd.astype(out_ref.dtype)
            if (at + 1) % step == 0:
                span = pl.ds(at + 1 - step, step)
                for half in range(2):
                    copies.append(
                        pltpu.make_async_copy(
                            out_ref.at[half, which, span],
                            out_hbm.at[half, which, span],
                            sems.at[half, which, at // step],
                        )
                    )
                    copies[-1].start()
    for copy in copies:
        copy.wait()


def pick(spread, partner):
    _, depth, bands = spread.shape
    shape = (2,) + partner.shape + (depth, bands // 2)
    return pl.pallas_call(
        pick_kernel,
        grid_spec=pltpu.PrefetchScalarGridSpec(
            num_scalar_prefetch=1,
            grid=(),
            in_specs=[WHOLE],
            out_specs=pl.BlockSpec(memory_space=pltpu.HBM),
            scratch_shapes=[pltpu.VMEM(shape, spread.dtype), pltpu.SemaphoreType.DMA((2, partner.shape[0], 4))],
        ),
        out_shape=pltpu.HBM(shape, spread.dtype),
        compiler_params=PARAMS,
        name="pick",
    )(partner, near(spread))


def turn(fetched_ref, left_ref):
    rows = fetched_ref.shape[0] // 2
    bands = fetched_ref.shape[1]
    turned = fetched_ref[...].T
    left_ref[:bands] = turned
    left_ref[bands:, :rows] = -turned[:, rows:]
    left_ref[bands:, rows:] = turned[:, :rows]


def couple_kernel(place_ref, fetched_hbm, own_ref, *refs):
    sides = fetched_hbm.shape[0]
    others_hbm, refs = refs[: sides - 1], refs[sides - 1 :]
    out_ref, fetched_ref, left_ref, sum_ref, others_ref, sems = refs
    pieces, rows, width = out_ref.shape
    block = width // 6
    incoming = [
        pltpu.make_async_copy(
            fetched_hbm.at[lax.bitwise_xor(place_ref[0], side)], fetched_ref.at[side], sems.at[0, side]
        )
        for side in range(sides)
    ]
    weights = [None] + [
        pltpu.make_async_copy(others_hbm[side - 1], others_ref.at[side - 1], sems.at[1, side])
        for side in range(1, sides)
    ]
    for copy in incoming[:2] + weights[1:2] + incoming[2:] + weights[2:3]:
        copy.start()
    for side in range(sides):
        incoming[side].wait()
        turn(fetched_ref.at[side], left_ref.at[side])
        if side:
            weights[side].wait()
            if side + 2 < sides:
                weights[side + 2].start()
        weighted_ref = others_ref.at[side - 1] if side else own_ref
        for start in range(0, width // 2, block):
            cols = slice(start, start + block)
            total = jnp.dot(left_ref[side], weighted_ref[:, cols], preferred_element_type=jnp.float32)
            if side:
                total += sum_ref[:, cols]
            if side < sides - 1:
                sum_ref[:, cols] = total
                continue
            total = total.astype(out_ref.dtype).reshape(2, pieces, rows, block)
            for part in range(2):
                at = 2 * start + part * block
                out_ref[:, :, at : at + block] = total[part]


def couple(place, fetched, own, others):
    sides, depth, bands = fetched.shape
    width = own.shape[-1]
    pieces = lax.axis_size(REDUCE)
    far_spec = pl.BlockSpec(memory_space=pltpu.HBM)
    return pl.pallas_call(
        couple_kernel,
        grid_spec=pltpu.PrefetchScalarGridSpec(
            num_scalar_prefetch=1,
            grid=(),
            in_specs=[far_spec, WHOLE] + [far_spec] * len(others),
            out_specs=WHOLE,
            scratch_shapes=[
                pltpu.VMEM(fetched.shape, fetched.dtype),
                pltpu.VMEM((sides, 2 * bands, depth), jnp.bfloat16),
                pltpu.VMEM((2 * bands, width), jnp.float32),
                pltpu.VMEM((len(others),) + own.shape, own.dtype),
                pltpu.SemaphoreType.DMA((2, sides)),
            ],
        ),
        out_shape=pltpu.VMEM((pieces, bands // pieces, 2 * width), jnp.bfloat16),
        compiler_params=PARAMS,
        name="couple",
    )(place.astype(jnp.int32).reshape(1), far(fetched), near(own), *[far(other) for other in others])


def final_kernel(parts_ref, out_ref):
    rows, num_q, modes, _, _, bands = out_ref.shape
    for which in range(num_q):
        for col in range(2 * modes):
            cols = slice(col * bands, (col + 1) * bands)
            total = parts_ref[which, :, cols].astype(jnp.float32)
            for source in range(which + num_q, parts_ref.shape[0], num_q):
                total = total + parts_ref[source, :, cols].astype(jnp.float32)
            for row in range(rows):
                out_ref[row, which, col // 2, col % 2] = total[row : row + 1]


def final(parts, num_q, modes):
    _, rows, width = parts.shape
    return pl.pallas_call(
        final_kernel,
        in_specs=[WHOLE],
        out_specs=WHOLE,
        out_shape=jax.ShapeDtypeStruct((rows, num_q, modes, 2, 1, width // (2 * modes)), jnp.float32),
        compiler_params=PARAMS,
        name="final",
    )(near(parts))


def exchange(value, axis):
    return lax.all_to_all(value, axis, split_axis=0, concat_axis=0, tiled=True)


def swap(value, axis):
    return lax.ppermute(value, axis, [(0, 1), (1, 0)])


def per_device(orbitals, fields, partner):
    num_q, modes = fields.shape[:2]
    own = orbitals[0]
    rows, bands = own.shape[1:]
    points = lax.axis_size(KA)
    depth = 2 * rows // points
    core = lax.axis_index("core")

    def of_q(values, which):
        return lax.dynamic_index_in_dim(values, which, 0, keepdims=False)

    spread = exchange(own.reshape(points, depth, bands), KA)
    across = swap(own, "xlo")
    across_fields = swap(fields, "xlo")
    beside = swap(own, "core")
    beside_field = swap(of_q(fields, 1 - core), "core")
    corner = swap(across, "core")
    corner_field = swap(of_q(across_fields, 1 - core), "core")
    own_weighted = weigh(of_q(fields, core), own)
    beside_weighted = weigh(beside_field, beside)
    across_weighted = weigh(of_q(across_fields, core), across)
    corner_weighted = weigh(corner_field, corner)
    picked = pick(spread, partner)
    fetched = exchange(picked.reshape(2 * num_q * points, depth, bands // 2), TEAM + KA)
    product = couple(
        lax.axis_index(TEAM),
        fetched.reshape(2 * num_q, 2 * rows, bands // 2),
        own_weighted,
        [beside_weighted, across_weighted, corner_weighted],
    )
    parts = exchange(product, REDUCE)
    return final(parts, num_q, modes)


def solution(mesh):
    fine = Mesh(mesh.devices.reshape(2, 8, 2, 2, 4, 2), KA + GRID)

    return jax.shard_map(
        per_device,
        mesh=fine,
        in_specs=(P(KA, None, GRID, None), P(None, None, None, GRID), P()),
        out_specs=P(GRID, None, None, None, KA, None),
        check_vma=False,
    )
```

time: 141 us -> 154 us (1.092)
  the two profiles are of different devices: /device:TPU:8 before, /device:TPU:1 now
where the time goes in v4:
time: 154 us; the launch traced here: 153 us
  blocking collectives  59.5 us (39%)
  waiting for transfers between devices  38.3 us (25%)
  starting transfers between devices  27.9 us (18%)
  Pallas kernels  24.7 us (16%)
  local copies, waits for them, and re-layouts  2.44 us (2%)
    all_to_all x2, blocking collectives, exchange(): return lax.all_to_all(value, axis, split_axis=0, concat_axis=0, tiled=True)  59.5 us
    ppermute x6, waiting for transfers between devices, swap(): return lax.ppermute(value, axis, [(0, 1), (1, 0)])  38.3 us
    ppermute x6, starting transfers between devices, swap(): return lax.ppermute(value, axis, [(0, 1), (1, 0)])  17.9 us
    pallas_call x4, Pallas kernels, weigh(): pl.pallas_call(weigh_kernel, grid=(rows // block,), in_specs=[pl.BlockSpe...  14.8 us
    all_to_all x1, starting transfers between devices, exchange(): return lax.all_to_all(value, axis, split_axis=0, concat_axis=0, tiled=True)  10 us
    pallas_call x1, Pallas kernels, couple(): pl.pallas_call(couple_kernel, grid_spec=pltpu.PrefetchScalarGridSpec(num_...  6.95 us
  transfers between devices with their start and end apart: 7, of which 1 were waited for; matrix products, arithmetic and copies ran while one was open for 1% of the time, Pallas kernels for 10%

profile of v4, /device:TPU:1, one launch (start us, length us, event | category | flops | bytes accessed | tf_op | source)
XLA Modules:
  0.0 153.1 jit_solution(16708199333709721134)
XLA Ops:
  0.0 36.5 %all_to_all.15.spread_ref = bf16[16,128,256]{2,1,0:T(8,128)(2,1)S(1)} all-to-all(bf16[16,128,256]{2,1,0:T(8,128)(2,1)} %bitcast.18), channel_id=1, replica_groups=mesh['ylo'=2,'z'=8,'xhi'=2,'xlo'=2,'yhi'=4,'core'=2] {'ylo','z'}, dimensions={0} | all-to-all | bytes 2097152 | tf_op jit(solution)/shard_map/all_to_all | solution.py:204
  36.5 0.7 copy-done.3
  37.2 2.2 %pick.1 = bf16[2,2,16,128,128]{4,3,2,1,0:T(8,128)(2,1)} custom-call(s32[2,16]{1,0:T(2,128)S(1)} %copy-done.3, bf16[16,128,256]{2,1,0:T(8,128)(2,1)S(1)} %all_to_all.15.spread_ref), custom_call_target="tpu_custom_call" | custom-call | tf_op jit(solution)/shard_map/pick/pallas_call | solution.py:89
  39.4 10.0 %all-to-all-start.1 = ((bf16[64,128,128]{2,1,0:T(8,128)(2,1)}), bf16[64,128,128]{2,1,0:T(8,128)(2,1)}, u32[]{:S(2)}, u32[]{:S(2)}) async-start(bf16[64,128,128]{2,1,0:T(8,128)(2,1)} %bitcast.29), calls=%async_computation.1 | async-start | bytes 4194304 | tf_op jit(solution)/shard_map/all_to_all | solution.py:204
  49.4 3.5 %collective-permute-start.3 = (bf16[2,1024,256]{2,1,0:T(8,128)(2,1)S(1)}, bf16[2,1024,256]{2,1,0:T(8,128)(2,1)}, u32[]{:S(2)}, u32[]{:S(2)}) collective-permute-start(bf16[2,1024,256]{2,1,0:T(8,128)(2,1)S(1)} %bitcast.19), channel_id=1, source_target_pairs={{0,8},{8,0},{1,9},{9,1},{2,10},{10,2},{3,11},{11,3},{4,12},{12,4},... | collective-permute-start | bytes 3145736 | tf_op jit(solution)/shard_map/ppermute | solution.py:208
  52.9 2.5 %collective-permute-start.1 = (bf16[2,1024,256]{2,1,0:T(8,128)(2,1)S(1)}, bf16[2,1024,256]{2,1,0:T(8,128)(2,1)S(1)}, u32[]{:S(2)}, u32[]{:S(2)}) collective-permute-start(bf16[2,1024,256]{2,1,0:T(8,128)(2,1)S(1)} %bitcast.20), channel_id=1, source_target_pairs={{0,1},{1,0},{2,3},{3,2},{4,5},{5,4},{6,7},{7,6},{8,9},{9,8},{10,11... | collective-permute-start | bytes 3145736 | tf_op jit(solution)/shard_map/ppermute | solution.py:208
  55.4 38.3 %collective-permute-done.3.own_ref = bf16[2,1024,256]{2,1,0:T(8,128)(2,1)} collective-permute-done((bf16[2,1024,256]{2,1,0:T(8,128)(2,1)S(1)}, bf16[2,1024,256]{2,1,0:T(8,128)(2,1)}, u32[]{:S(2)}, u32[]{:S(2)}) %collective-permute-start.3) | collective-permute-done | bytes 1048608 | tf_op jit(solution)/shard_map/ppermute | solution.py:208
  93.7 3.1 %collective-permute-start.5 = (bf16[2,1024,256]{2,1,0:T(8,128)(2,1)}, bf16[2,1024,256]{2,1,0:T(8,128)(2,1)}, u32[]{:S(2)}, u32[]{:S(2)}) collective-permute-start(bf16[2,1024,256]{2,1,0:T(8,128)(2,1)} %collective-permute-done.3.own_ref), channel_id=1, source_target_pairs={{0,1},{1,0},{2,3},{3,2},{4,5},{5,4},{6,7},{7,6},{8,9},{9,8},{10,11... | collective-permute-start | bytes 3145736 | tf_op jit(solution)/shard_map/ppermute | solution.py:208
  96.8 4.5 %collective-permute-start.2 = (bf16[2,3,2,1024]{3,2,1,0:T(2,128)(2,1)S(1)}, bf16[2,3,2,1024]{3,2,1,0:T(2,128)(2,1)S(1)}, u32[]{:S(2)}, u32[]{:S(2)}) collective-permute-start(bf16[2,3,2,1024]{3,2,1,0:T(2,128)(2,1)S(1)} %copy-done.4), channel_id=1, source_target_pairs={{0,8},{8,0},{1,9},{9,1},{2,10},{10,2},{3,11},{11,3},{4,12},{12,4},... | collective-permute-start | bytes 73736 | tf_op jit(solution)/shard_map/ppermute | solution.py:208
  101.4 2.2 %collective-permute-start = (bf16[3,2,1024]{2,1,0:T(2,128)(2,1)S(1)}, bf16[3,2,1024]{2,1,0:T(2,128)(2,1)S(1)}, u32[]{:S(2)}, u32[]{:S(2)}) collective-permute-start(bf16[3,2,1024]{2,1,0:T(2,128)(2,1)S(1)} %get-tuple-element.7), channel_id=1, source_target_pairs={{0,1},{1,0},{2,3},{3,2},{4,5},{5,4},{6,7},{7,6},{8,9},{9,8},{10,11... | collective-permute-start | bytes 36872 | tf_op jit(solution)/shard_map/ppermute | solution.py:208
  103.6 2.1 %collective-permute-start.4 = (bf16[3,2,1024]{2,1,0:T(2,128)(2,1)S(1)}, bf16[3,2,1024]{2,1,0:T(2,128)(2,1)S(1)}, u32[]{:S(2)}, u32[]{:S(2)}) collective-permute-start(bf16[3,2,1024]{2,1,0:T(2,128)(2,1)S(1)} %get-tuple-element.5), channel_id=1, source_target_pairs={{0,1},{1,0},{2,3},{3,2},{4,5},{5,4},{6,7},{7,6},{8,9},{9,8},{10,11... | collective-permute-start | bytes 36872 | tf_op jit(solution)/shard_map/ppermute | solution.py:208
  105.8 0.2 copy.6
  106.0 2.9 %weigh.4 = bf16[2,1024,768]{2,1,0:T(8,128)(2,1)} custom-call(f32[1024,6]{1,0:T(8,128)S(1)} %bitcast.25, bf16[2,1024,256]{2,1,0:T(8,128)(2,1)S(1)} %bitcast.21), custom_call_target="tpu_custom_call" | custom-call | tf_op jit(solution)/shard_map/weigh/pallas_call | solution.py:41
  108.9 0.2 copy.7
  109.2 0.2 copy.8
  109.4 1.0 copy.9
  110.5 4.4 %weigh.6 = bf16[2,1024,768]{2,1,0:T(8,128)(2,1)} custom-call(f32[1024,6]{1,0:T(8,128)S(1)} %bitcast.24, bf16[2,1024,256]{2,1,0:T(8,128)(2,1)} %collective-permute-done.3.own_ref), custom_call_target="tpu_custom_call" | custom-call | tf_op jit(solution)/shard_map/weigh/pallas_call | solution.py:41
  114.9 2.9 %weigh.5 = bf16[2,1024,768]{2,1,0:T(8,128)(2,1)} custom-call(f32[1024,6]{1,0:T(8,128)S(1)} %bitcast.22, bf16[2,1024,256]{2,1,0:T(8,128)(2,1)S(1)} %collective-permute-done.1.own_ref), custom_call_target="tpu_custom_call" | custom-call | tf_op jit(solution)/shard_map/weigh/pallas_call | solution.py:41
  117.8 0.0 collective-permute-done.5.own_ref
  117.8 4.5 %weigh.7 = bf16[2,1024,768]{2,1,0:T(8,128)(2,1)} custom-call(f32[1024,6]{1,0:T(8,128)S(1)} %bitcast.23, bf16[2,1024,256]{2,1,0:T(8,128)(2,1)} %collective-permute-done.5.own_ref), custom_call_target="tpu_custom_call" | custom-call | tf_op jit(solution)/shard_map/weigh/pallas_call | solution.py:41
  122.4 0.0 all-to-all-done.1
  122.4 6.9 %couple.1 = bf16[16,8,1536]{2,1,0:T(8,128)(2,1)S(1)} custom-call(s32[1]{0:T(128)} %bitcast.place_ref, bf16[4,2048,128]{2,1,0:T(8,128)(2,1)} %bitcast.3.fetched_hbm, bf16[2048,768]{1,0:T(8,128)(2,1)S(1)} %bitcast.17, bf16[2048,768]{1,0:T(8,128)(2,1)} %bitcast.27, bf16[2048,768]{1,0:T(8,128)(2,1)} %bitcast.26, bf16[2048,768]{1,0:T(8,128)(2,1)} %bitcast.28), custom_call_target="tpu_custom_call" | custom-call | tf_op jit(solution)/shard_map/couple/pallas_call | solution.py:158
  129.3 23.0 %all_to_all.16.parts_ref = bf16[16,8,1536]{2,1,0:T(8,128)(2,1)S(1)} all-to-all(bf16[16,8,1536]{2,1,0:T(8,128)(2,1)S(1)} %couple.1), channel_id=1, replica_groups=mesh['ylo'=2,'z'=8,'xhi'=2,'xlo'=2,'yhi'=4,'core'=2] {'xhi','yhi','core'}, dimensions={0} | all-to-all | bytes 786432 | tf_op jit(solution)/shard_map/all_to_all | solution.py:204
  152.4 0.7 final.1
  (19 shorter events, 0.1 us)
Async XLA Ops:
  36.5 0.7 copy-start.3
  37.2 12.2 %copy-start.1 = (bf16[1,2,1024,256]{3,2,1,0:T(8,128)(2,1)S(1)}, bf16[1,2,1024,256]{3,2,1,0:T(8,128)(2,1)}, u32[]{:S(2)}) copy-start(bf16[1,2,1024,256]{3,2,1,0:T(8,128)(2,1)} %param.3) | copy-start | bytes 3145732
  37.2 59.6 %copy-start.4 = (bf16[2,3,2,1024]{3,2,1,0:T(2,128)(2,1)S(1)}, bf16[2,3,2,1024]{3,2,1,0:T(2,128)(2,1)}, u32[]{:S(2)}) copy-start(bf16[2,3,2,1024]{3,2,1,0:T(2,128)(2,1)} %param.4) | copy-start | bytes 73732
  39.4 83.0 %all-to-all-start.1 = ((bf16[64,128,128]{2,1,0:T(8,128)(2,1)}), bf16[64,128,128]{2,1,0:T(8,128)(2,1)}, u32[]{:S(2)}, u32[]{:S(2)}) async-start(bf16[64,128,128]{2,1,0:T(8,128)(2,1)} %bitcast.29), calls=%async_computation.1 | async-start | bytes 4194304 | tf_op jit(solution)/shard_map/all_to_all | solution.py:204
  49.4 44.2 %collective-permute-start.3 = (bf16[2,1024,256]{2,1,0:T(8,128)(2,1)S(1)}, bf16[2,1024,256]{2,1,0:T(8,128)(2,1)}, u32[]{:S(2)}, u32[]{:S(2)}) collective-permute-start(bf16[2,1024,256]{2,1,0:T(8,128)(2,1)S(1)} %bitcast.19), channel_id=1, source_target_pairs={{0,8},{8,0},{1,9},{9,1},{2,10},{10,2},{3,11},{11,3},{4,12},{12,4},... | collective-permute-start | bytes 3145736 | tf_op jit(solution)/shard_map/ppermute | solution.py:208
  52.9 62.0 %collective-permute-start.1 = (bf16[2,1024,256]{2,1,0:T(8,128)(2,1)S(1)}, bf16[2,1024,256]{2,1,0:T(8,128)(2,1)S(1)}, u32[]{:S(2)}, u32[]{:S(2)}) collective-permute-start(bf16[2,1024,256]{2,1,0:T(8,128)(2,1)S(1)} %bitcast.20), channel_id=1, source_target_pairs={{0,1},{1,0},{2,3},{3,2},{4,5},{5,4},{6,7},{7,6},{8,9},{9,8},{10,11... | collective-permute-start | bytes 3145736 | tf_op jit(solution)/shard_map/ppermute | solution.py:208
  93.7 24.2 %collective-permute-start.5 = (bf16[2,1024,256]{2,1,0:T(8,128)(2,1)}, bf16[2,1024,256]{2,1,0:T(8,128)(2,1)}, u32[]{:S(2)}, u32[]{:S(2)}) collective-permute-start(bf16[2,1024,256]{2,1,0:T(8,128)(2,1)} %collective-permute-done.3.own_ref), channel_id=1, source_target_pairs={{0,1},{1,0},{2,3},{3,2},{4,5},{5,4},{6,7},{7,6},{8,9},{9,8},{10,11... | collective-permute-start | bytes 3145736 | tf_op jit(solution)/shard_map/ppermute | solution.py:208
  96.8 6.8 %collective-permute-start.2 = (bf16[2,3,2,1024]{3,2,1,0:T(2,128)(2,1)S(1)}, bf16[2,3,2,1024]{3,2,1,0:T(2,128)(2,1)S(1)}, u32[]{:S(2)}, u32[]{:S(2)}) collective-permute-start(bf16[2,3,2,1024]{3,2,1,0:T(2,128)(2,1)S(1)} %copy-done.4), channel_id=1, source_target_pairs={{0,8},{8,0},{1,9},{9,1},{2,10},{10,2},{3,11},{11,3},{4,12},{12,4},... | collective-permute-start | bytes 73736 | tf_op jit(solution)/shard_map/ppermute | solution.py:208
  101.4 7.5 %collective-permute-start = (bf16[3,2,1024]{2,1,0:T(2,128)(2,1)S(1)}, bf16[3,2,1024]{2,1,0:T(2,128)(2,1)S(1)}, u32[]{:S(2)}, u32[]{:S(2)}) collective-permute-start(bf16[3,2,1024]{2,1,0:T(2,128)(2,1)S(1)} %get-tuple-element.7), channel_id=1, source_target_pairs={{0,1},{1,0},{2,3},{3,2},{4,5},{5,4},{6,7},{7,6},{8,9},{9,8},{10,11... | collective-permute-start | bytes 36872 | tf_op jit(solution)/shard_map/ppermute | solution.py:208
  103.6 5.8 %collective-permute-start.4 = (bf16[3,2,1024]{2,1,0:T(2,128)(2,1)S(1)}, bf16[3,2,1024]{2,1,0:T(2,128)(2,1)S(1)}, u32[]{:S(2)}, u32[]{:S(2)}) collective-permute-start(bf16[3,2,1024]{2,1,0:T(2,128)(2,1)S(1)} %get-tuple-element.5), channel_id=1, source_target_pairs={{0,1},{1,0},{2,3},{3,2},{4,5},{5,4},{6,7},{7,6},{8,9},{9,8},{10,11... | collective-permute-start | bytes 36872 | tf_op jit(solution)/shard_map/ppermute | solution.py:208
  114.9 2.9 %copy-start.2 = (f32[6,1024]{0,1:T(8,128)S(1)}, f32[6,1024]{0,1:T(8,128)}, u32[]{:S(2)}) copy-start(f32[6,1024]{0,1:T(8,128)} %copy.9) | copy-start | bytes 73732
  117.8 4.5 %copy-start = (bf16[2,1024,768]{2,1,0:T(8,128)(2,1)S(1)}, bf16[2,1024,768]{2,1,0:T(8,128)(2,1)}, u32[]{:S(2)}) copy-start(bf16[2,1024,768]{2,1,0:T(8,128)(2,1)} %weigh.4) | copy-start | bytes 9437188

commit v5 on v4

--- a/solution.py
+++ b/solution.py
@@ -54,38 +54,32 @@
 
 
 def pick_kernel(partner_ref, spread_ref, out_hbm, out_ref, sems):
-    num_q, points = out_ref.shape[1:3]
+    points, _, num_q = out_ref.shape[:3]
     lanes = out_ref.shape[-1]
     quarter = lanes // 2
-    step = points // 4
+    step = points // sems.shape[0]
     low = lax.broadcasted_iota(jnp.int32, out_ref.shape[3:], 1) < quarter
     copies = []
-    for which in range(num_q):
-        for at in range(points):
+    for at in range(points):
+        for which in range(num_q):
             block = spread_ref[partner_ref[which, at]].astype(jnp.float32)
             left, right = block[:, :lanes], block[:, lanes:]
             even = jnp.where(low, left, pltpu.roll(right, quarter, 1))
             odd = jnp.where(low, pltpu.roll(left, quarter, 1), right)
-            out_ref[0, which, at] = even.astype(out_ref.dtype)
-            out_ref[1, which, at] = odd.astype(out_ref.dtype)
-            if (at + 1) % step == 0:
-                span = pl.ds(at + 1 - step, step)
-                for half in range(2):
-                    copies.append(
-                        pltpu.make_async_copy(
-                            out_ref.at[half, which, span],
-                            out_hbm.at[half, which, span],
-                            sems.at[half, which, at // step],
-                        )
-                    )
-                    copies[-1].start()
+            out_ref[at, 0, which] = even.astype(out_ref.dtype)
+            out_ref[at, 1, which] = odd.astype(out_ref.dtype)
+        if (at + 1) % step == 0:
+            span = pl.ds(at + 1 - step, step)
+            copies.append(pltpu.make_async_copy(out_ref.at[span], out_hbm.at[span], sems.at[at // step]))
+            copies[-1].start()
     for copy in copies:
         copy.wait()
 
 
 def pick(spread, partner):
     _, depth, bands = spread.shape
-    shape = (2,) + partner.shape + (depth, bands // 2)
+    num_q, points = partner.shape
+    shape = (points, 2, num_q, depth, bands // 2)
     return pl.pallas_call(
         pick_kernel,
         grid_spec=pltpu.PrefetchScalarGridSpec(
@@ -93,7 +87,7 @@
             grid=(),
             in_specs=[WHOLE],
             out_specs=pl.BlockSpec(memory_space=pltpu.HBM),
-            scratch_shapes=[pltpu.VMEM(shape, spread.dtype), pltpu.SemaphoreType.DMA((2, partner.shape[0], 4))],
+            scratch_shapes=[pltpu.VMEM(shape, spread.dtype), pltpu.SemaphoreType.DMA((8,))],
         ),
         out_shape=pltpu.HBM(shape, spread.dtype),
         compiler_params=PARAMS,
@@ -102,23 +96,23 @@
 
 
 def turn(fetched_ref, left_ref):
-    rows = fetched_ref.shape[0] // 2
-    bands = fetched_ref.shape[1]
-    turned = fetched_ref[...].T
+    bands = fetched_ref.shape[-1]
+    turned = fetched_ref[...].reshape(-1, bands).T
+    rows = turned.shape[1] // 2
     left_ref[:bands] = turned
     left_ref[bands:, :rows] = -turned[:, rows:]
     left_ref[bands:, rows:] = turned[:, :rows]
 
 
 def couple_kernel(place_ref, fetched_hbm, own_ref, *refs):
-    sides = fetched_hbm.shape[0]
+    sides = fetched_hbm.shape[1]
     others_hbm, refs = refs[: sides - 1], refs[sides - 1 :]
     out_ref, fetched_ref, left_ref, sum_ref, others_ref, sems = refs
     pieces, rows, width = out_ref.shape
     block = width // 6
     incoming = [
         pltpu.make_async_copy(
-            fetched_hbm.at[lax.bitwise_xor(place_ref[0], side)], fetched_ref.at[side], sems.at[0, side]
+            fetched_hbm.at[:, lax.bitwise_xor(place_ref[0], side)], fetched_ref.at[side], sems.at[0, side]
         )
         for side in range(sides)
     ]
@@ -151,7 +145,7 @@
 
 
 def couple(place, fetched, own, others):
-    sides, depth, bands = fetched.shape
+    points, sides, depth, bands = fetched.shape
     width = own.shape[-1]
     pieces = lax.axis_size(REDUCE)
     far_spec = pl.BlockSpec(memory_space=pltpu.HBM)
@@ -163,8 +157,8 @@
             in_specs=[far_spec, WHOLE] + [far_spec] * len(others),
             out_specs=WHOLE,
             scratch_shapes=[
-                pltpu.VMEM(fetched.shape, fetched.dtype),
-                pltpu.VMEM((sides, 2 * bands, depth), jnp.bfloat16),
+                pltpu.VMEM((sides, points, depth, bands), fetched.dtype),
+                pltpu.VMEM((sides, 2 * bands, points * depth), jnp.bfloat16),
                 pltpu.VMEM((2 * bands, width), jnp.float32),
                 pltpu.VMEM((len(others),) + own.shape, own.dtype),
                 pltpu.SemaphoreType.DMA((2, sides)),
@@ -231,10 +225,10 @@
     across_weighted = weigh(of_q(across_fields, core), across)
     corner_weighted = weigh(corner_field, corner)
     picked = pick(spread, partner)
-    fetched = exchange(picked.reshape(2 * num_q * points, depth, bands // 2), TEAM + KA)
+    fetched = exchange(picked.reshape(points * 2 * num_q, depth, bands // 2), KA + TEAM)
     product = couple(
         lax.axis_index(TEAM),
-        fetched.reshape(2 * num_q, 2 * rows, bands // 2),
+        fetched.reshape(points, 2 * num_q, depth, bands // 2),
         own_weighted,
         [beside_weighted, across_weighted, corner_weighted],
     )

time: 154 us -> 155 us (level)
  waiting for transfers between devices: 38.3 us -> 41.1 us
  starting transfers between devices: 27.9 us -> 26.3 us
    ppermute x6, waiting for transfers between devices: 38.3 us -> 41.1 us  [swap(): return lax.ppermute(value, axis, [(0, 1), (1, 0)])]
    ppermute x6, starting transfers between devices: 17.9 us -> 16.3 us  [swap(): return lax.ppermute(value, axis, [(0, 1), (1, 0)])]
where the time goes in v5:
time: 155 us; the launch traced here: 154 us
  blocking collectives  59.4 us (38%)
  waiting for transfers between devices  41.1 us (27%)
  starting transfers between devices  26.3 us (17%)
  Pallas kernels  24.6 us (16%)
  local copies, waits for them, and re-layouts  2.44 us (2%)
    all_to_all x2, blocking collectives, exchange(): return lax.all_to_all(value, axis, split_axis=0, concat_axis=0, tiled=True)  59.4 us
    ppermute x6, waiting for transfers between devices, swap(): return lax.ppermute(value, axis, [(0, 1), (1, 0)])  41.1 us
    ppermute x6, starting transfers between devices, swap(): return lax.ppermute(value, axis, [(0, 1), (1, 0)])  16.3 us
    pallas_call x4, Pallas kernels, weigh(): pl.pallas_call(weigh_kernel, grid=(rows // block,), in_specs=[pl.BlockSpe...  14.8 us
    all_to_all x1, starting transfers between devices, exchange(): return lax.all_to_all(value, axis, split_axis=0, concat_axis=0, tiled=True)  9.99 us
    pallas_call x1, Pallas kernels, couple(): pl.pallas_call(couple_kernel, grid_spec=pltpu.PrefetchScalarGridSpec(num_...  6.95 us
  transfers between devices with their start and end apart: 7, of which 1 were waited for; matrix products, arithmetic and copies ran while one was open for 1% of the time, Pallas kernels for 10%

profile of v5, /device:TPU:1, one launch (start us, length us, event | category | flops | bytes accessed | tf_op | source)
XLA Modules:
  0.0 154.0 jit_solution(3015000082697869769)
XLA Ops:
  0.0 36.5 %all_to_all.15.spread_ref = bf16[16,128,256]{2,1,0:T(8,128)(2,1)S(1)} all-to-all(bf16[16,128,256]{2,1,0:T(8,128)(2,1)} %bitcast.18), channel_id=1, replica_groups=mesh['ylo'=2,'z'=8,'xhi'=2,'xlo'=2,'yhi'=4,'core'=2] {'ylo','z'}, dimensions={0} | all-to-all | bytes 2097152 | tf_op jit(solution)/shard_map/all_to_all | solution.py:198
  36.5 0.7 copy-done.3
  37.2 2.1 %pick.1 = bf16[16,2,2,128,128]{4,3,2,1,0:T(8,128)(2,1)} custom-call(s32[2,16]{1,0:T(2,128)S(1)} %copy-done.3, bf16[16,128,256]{2,1,0:T(8,128)(2,1)S(1)} %all_to_all.15.spread_ref), custom_call_target="tpu_custom_call" | custom-call | tf_op jit(solution)/shard_map/pick/pallas_call | solution.py:83
  39.3 10.0 %all-to-all-start.1 = ((bf16[64,128,128]{2,1,0:T(8,128)(2,1)}), bf16[64,128,128]{2,1,0:T(8,128)(2,1)}, u32[]{:S(2)}, u32[]{:S(2)}) async-start(bf16[64,128,128]{2,1,0:T(8,128)(2,1)} %bitcast.29), calls=%async_computation.1 | async-start | bytes 4194304 | tf_op jit(solution)/shard_map/all_to_all | solution.py:198
  49.4 3.3 %collective-permute-start.3 = (bf16[2,1024,256]{2,1,0:T(8,128)(2,1)S(1)}, bf16[2,1024,256]{2,1,0:T(8,128)(2,1)}, u32[]{:S(2)}, u32[]{:S(2)}) collective-permute-start(bf16[2,1024,256]{2,1,0:T(8,128)(2,1)S(1)} %bitcast.19), channel_id=1, source_target_pairs={{0,8},{8,0},{1,9},{9,1},{2,10},{10,2},{3,11},{11,3},{4,12},{12,4},... | collective-permute-start | bytes 3145736 | tf_op jit(solution)/shard_map/ppermute | solution.py:202
  52.6 2.6 %collective-permute-start.1 = (bf16[2,1024,256]{2,1,0:T(8,128)(2,1)S(1)}, bf16[2,1024,256]{2,1,0:T(8,128)(2,1)S(1)}, u32[]{:S(2)}, u32[]{:S(2)}) collective-permute-start(bf16[2,1024,256]{2,1,0:T(8,128)(2,1)S(1)} %bitcast.20), channel_id=1, source_target_pairs={{0,1},{1,0},{2,3},{3,2},{4,5},{5,4},{6,7},{7,6},{8,9},{9,8},{10,11... | collective-permute-start | bytes 3145736 | tf_op jit(solution)/shard_map/ppermute | solution.py:202
  55.2 41.1 %collective-permute-done.3.own_ref = bf16[2,1024,256]{2,1,0:T(8,128)(2,1)} collective-permute-done((bf16[2,1024,256]{2,1,0:T(8,128)(2,1)S(1)}, bf16[2,1024,256]{2,1,0:T(8,128)(2,1)}, u32[]{:S(2)}, u32[]{:S(2)}) %collective-permute-start.3) | collective-permute-done | bytes 1048608 | tf_op jit(solution)/shard_map/ppermute | solution.py:202
  96.3 2.9 %collective-permute-start.5 = (bf16[2,1024,256]{2,1,0:T(8,128)(2,1)}, bf16[2,1024,256]{2,1,0:T(8,128)(2,1)}, u32[]{:S(2)}, u32[]{:S(2)}) collective-permute-start(bf16[2,1024,256]{2,1,0:T(8,128)(2,1)} %collective-permute-done.3.own_ref), channel_id=1, source_target_pairs={{0,1},{1,0},{2,3},{3,2},{4,5},{5,4},{6,7},{7,6},{8,9},{9,8},{10,11... | collective-permute-start | bytes 3145736 | tf_op jit(solution)/shard_map/ppermute | solution.py:202
  99.2 2.6 %collective-permute-start.2 = (bf16[2,3,2,1024]{3,2,1,0:T(2,128)(2,1)S(1)}, bf16[2,3,2,1024]{3,2,1,0:T(2,128)(2,1)S(1)}, u32[]{:S(2)}, u32[]{:S(2)}) collective-permute-start(bf16[2,3,2,1024]{3,2,1,0:T(2,128)(2,1)S(1)} %copy-done.4), channel_id=1, source_target_pairs={{0,8},{8,0},{1,9},{9,1},{2,10},{10,2},{3,11},{11,3},{4,12},{12,4},... | collective-permute-start | bytes 73736 | tf_op jit(solution)/shard_map/ppermute | solution.py:202
  101.8 2.2 %collective-permute-start = (bf16[3,2,1024]{2,1,0:T(2,128)(2,1)S(1)}, bf16[3,2,1024]{2,1,0:T(2,128)(2,1)S(1)}, u32[]{:S(2)}, u32[]{:S(2)}) collective-permute-start(bf16[3,2,1024]{2,1,0:T(2,128)(2,1)S(1)} %get-tuple-element.7), channel_id=1, source_target_pairs={{0,1},{1,0},{2,3},{3,2},{4,5},{5,4},{6,7},{7,6},{8,9},{9,8},{10,11... | collective-permute-start | bytes 36872 | tf_op jit(solution)/shard_map/ppermute | solution.py:202
  104.1 2.8 %collective-permute-start.4 = (bf16[3,2,1024]{2,1,0:T(2,128)(2,1)S(1)}, bf16[3,2,1024]{2,1,0:T(2,128)(2,1)S(1)}, u32[]{:S(2)}, u32[]{:S(2)}) collective-permute-start(bf16[3,2,1024]{2,1,0:T(2,128)(2,1)S(1)} %get-tuple-element.5), channel_id=1, source_target_pairs={{0,1},{1,0},{2,3},{3,2},{4,5},{5,4},{6,7},{7,6},{8,9},{9,8},{10,11... | collective-permute-start | bytes 36872 | tf_op jit(solution)/shard_map/ppermute | solution.py:202
  106.9 0.2 copy.6
  107.1 2.9 %weigh.4 = bf16[2,1024,768]{2,1,0:T(8,128)(2,1)} custom-call(f32[1024,6]{1,0:T(8,128)S(1)} %bitcast.25, bf16[2,1024,256]{2,1,0:T(8,128)(2,1)S(1)} %bitcast.21), custom_call_target="tpu_custom_call" | custom-call | tf_op jit(solution)/shard_map/weigh/pallas_call | solution.py:41
  110.0 0.2 copy.7
  110.3 0.2 copy.8
  110.5 0.0 collective-permute-done.4
  110.5 1.0 copy.9
  111.6 4.4 %weigh.6 = bf16[2,1024,768]{2,1,0:T(8,128)(2,1)} custom-call(f32[1024,6]{1,0:T(8,128)S(1)} %bitcast.24, bf16[2,1024,256]{2,1,0:T(8,128)(2,1)} %collective-permute-done.3.own_ref), custom_call_target="tpu_custom_call" | custom-call | tf_op jit(solution)/shard_map/weigh/pallas_call | solution.py:41
  116.0 2.9 %weigh.5 = bf16[2,1024,768]{2,1,0:T(8,128)(2,1)} custom-call(f32[1024,6]{1,0:T(8,128)S(1)} %bitcast.22, bf16[2,1024,256]{2,1,0:T(8,128)(2,1)S(1)} %collective-permute-done.1.own_ref), custom_call_target="tpu_custom_call" | custom-call | tf_op jit(solution)/shard_map/weigh/pallas_call | solution.py:41
  118.9 0.0 collective-permute-done.5.own_ref
  118.9 4.5 %weigh.7 = bf16[2,1024,768]{2,1,0:T(8,128)(2,1)} custom-call(f32[1024,6]{1,0:T(8,128)S(1)} %bitcast.23, bf16[2,1024,256]{2,1,0:T(8,128)(2,1)} %collective-permute-done.5.own_ref), custom_call_target="tpu_custom_call" | custom-call | tf_op jit(solution)/shard_map/weigh/pallas_call | solution.py:41
  123.5 6.9 %couple.1 = bf16[16,8,1536]{2,1,0:T(8,128)(2,1)S(1)} custom-call(s32[1]{0:T(128)} %bitcast.place_ref, bf16[16,4,128,128]{3,2,1,0:T(8,128)(2,1)} %bitcast.3.fetched_hbm, bf16[2048,768]{1,0:T(8,128)(2,1)S(1)} %bitcast.17, bf16[2048,768]{1,0:T(8,128)(2,1)} %bitcast.27, bf16[2048,768]{1,0:T(8,128)(2,1)} %bitcast.26, bf16[2048,768]{1,0:T(8,128)(2,1)} %bitcast.28), custom_call_target="tpu_custom_call" | custom-call | tf_op jit(solution)/shard_map/couple/pallas_call | solution.py:152
  130.4 22.9 %all_to_all.16.parts_ref = bf16[16,8,1536]{2,1,0:T(8,128)(2,1)S(1)} all-to-all(bf16[16,8,1536]{2,1,0:T(8,128)(2,1)S(1)} %couple.1), channel_id=1, replica_groups=mesh['ylo'=2,'z'=8,'xhi'=2,'xlo'=2,'yhi'=4,'core'=2] {'xhi','yhi','core'}, dimensions={0} | all-to-all | bytes 786432 | tf_op jit(solution)/shard_map/all_to_all | solution.py:198
  153.3 0.7 final.1
  (19 shorter events, 0.1 us)
Async XLA Ops:
  36.5 0.7 copy-start.3
  37.2 12.2 %copy-start.1 = (bf16[1,2,1024,256]{3,2,1,0:T(8,128)(2,1)S(1)}, bf16[1,2,1024,256]{3,2,1,0:T(8,128)(2,1)}, u32[]{:S(2)}) copy-start(bf16[1,2,1024,256]{3,2,1,0:T(8,128)(2,1)} %param.3) | copy-start | bytes 3145732
  37.2 62.0 %copy-start.4 = (bf16[2,3,2,1024]{3,2,1,0:T(2,128)(2,1)S(1)}, bf16[2,3,2,1024]{3,2,1,0:T(2,128)(2,1)}, u32[]{:S(2)}) copy-start(bf16[2,3,2,1024]{3,2,1,0:T(2,128)(2,1)} %param.4) | copy-start | bytes 73732
  39.3 84.1 %all-to-all-start.1 = ((bf16[64,128,128]{2,1,0:T(8,128)(2,1)}), bf16[64,128,128]{2,1,0:T(8,128)(2,1)}, u32[]{:S(2)}, u32[]{:S(2)}) async-start(bf16[64,128,128]{2,1,0:T(8,128)(2,1)} %bitcast.29), calls=%async_computation.1 | async-start | bytes 4194304 | tf_op jit(solution)/shard_map/all_to_all | solution.py:198
  49.4 47.0 %collective-permute-start.3 = (bf16[2,1024,256]{2,1,0:T(8,128)(2,1)S(1)}, bf16[2,1024,256]{2,1,0:T(8,128)(2,1)}, u32[]{:S(2)}, u32[]{:S(2)}) collective-permute-start(bf16[2,1024,256]{2,1,0:T(8,128)(2,1)S(1)} %bitcast.19), channel_id=1, source_target_pairs={{0,8},{8,0},{1,9},{9,1},{2,10},{10,2},{3,11},{11,3},{4,12},{12,4},... | collective-permute-start | bytes 3145736 | tf_op jit(solution)/shard_map/ppermute | solution.py:202
  52.6 63.4 %collective-permute-start.1 = (bf16[2,1024,256]{2,1,0:T(8,128)(2,1)S(1)}, bf16[2,1024,256]{2,1,0:T(8,128)(2,1)S(1)}, u32[]{:S(2)}, u32[]{:S(2)}) collective-permute-start(bf16[2,1024,256]{2,1,0:T(8,128)(2,1)S(1)} %bitcast.20), channel_id=1, source_target_pairs={{0,1},{1,0},{2,3},{3,2},{4,5},{5,4},{6,7},{7,6},{8,9},{9,8},{10,11... | collective-permute-start | bytes 3145736 | tf_op jit(solution)/shard_map/ppermute | solution.py:202
  96.3 22.6 %collective-permute-start.5 = (bf16[2,1024,256]{2,1,0:T(8,128)(2,1)}, bf16[2,1024,256]{2,1,0:T(8,128)(2,1)}, u32[]{:S(2)}, u32[]{:S(2)}) collective-permute-start(bf16[2,1024,256]{2,1,0:T(8,128)(2,1)} %collective-permute-done.3.own_ref), channel_id=1, source_target_pairs={{0,1},{1,0},{2,3},{3,2},{4,5},{5,4},{6,7},{7,6},{8,9},{9,8},{10,11... | collective-permute-start | bytes 3145736 | tf_op jit(solution)/shard_map/ppermute | solution.py:202
  99.2 4.8 %collective-permute-start.2 = (bf16[2,3,2,1024]{3,2,1,0:T(2,128)(2,1)S(1)}, bf16[2,3,2,1024]{3,2,1,0:T(2,128)(2,1)S(1)}, u32[]{:S(2)}, u32[]{:S(2)}) collective-permute-start(bf16[2,3,2,1024]{3,2,1,0:T(2,128)(2,1)S(1)} %copy-done.4), channel_id=1, source_target_pairs={{0,8},{8,0},{1,9},{9,1},{2,10},{10,2},{3,11},{11,3},{4,12},{12,4},... | collective-permute-start | bytes 73736 | tf_op jit(solution)/shard_map/ppermute | solution.py:202
  101.8 8.2 %collective-permute-start = (bf16[3,2,1024]{2,1,0:T(2,128)(2,1)S(1)}, bf16[3,2,1024]{2,1,0:T(2,128)(2,1)S(1)}, u32[]{:S(2)}, u32[]{:S(2)}) collective-permute-start(bf16[3,2,1024]{2,1,0:T(2,128)(2,1)S(1)} %get-tuple-element.7), channel_id=1, source_target_pairs={{0,1},{1,0},{2,3},{3,2},{4,5},{5,4},{6,7},{7,6},{8,9},{9,8},{10,11... | collective-permute-start | bytes 36872 | tf_op jit(solution)/shard_map/ppermute | solution.py:202
  104.1 6.4 %collective-permute-start.4 = (bf16[3,2,1024]{2,1,0:T(2,128)(2,1)S(1)}, bf16[3,2,1024]{2,1,0:T(2,128)(2,1)S(1)}, u32[]{:S(2)}, u32[]{:S(2)}) collective-permute-start(bf16[3,2,1024]{2,1,0:T(2,128)(2,1)S(1)} %get-tuple-element.5), channel_id=1, source_target_pairs={{0,1},{1,0},{2,3},{3,2},{4,5},{5,4},{6,7},{7,6},{8,9},{9,8},{10,11... | collective-permute-start | bytes 36872 | tf_op jit(solution)/shard_map/ppermute | solution.py:202
  116.0 2.9 %copy-start.2 = (f32[6,1024]{0,1:T(8,128)S(1)}, f32[6,1024]{0,1:T(8,128)}, u32[]{:S(2)}) copy-start(f32[6,1024]{0,1:T(8,128)} %copy.9) | copy-start | bytes 73732
  118.9 4.5 %copy-start = (bf16[2,1024,768]{2,1,0:T(8,128)(2,1)S(1)}, bf16[2,1024,768]{2,1,0:T(8,128)(2,1)}, u32[]{:S(2)}) copy-start(bf16[2,1024,768]{2,1,0:T(8,128)(2,1)} %weigh.4) | copy-start | bytes 9437188

commit v6 on v5

--- a/solution.py
+++ b/solution.py
@@ -120,15 +120,15 @@
         pltpu.make_async_copy(others_hbm[side - 1], others_ref.at[side - 1], sems.at[1, side])
         for side in range(1, sides)
     ]
-    for copy in incoming[:2] + weights[1:2] + incoming[2:] + weights[2:3]:
-        copy.start()
+    for side in range(sides):
+        incoming[side].start()
+        if side:
+            weights[side].start()
     for side in range(sides):
         incoming[side].wait()
         turn(fetched_ref.at[side], left_ref.at[side])
         if side:
             weights[side].wait()
-            if side + 2 < sides:
-                weights[side + 2].start()
         weighted_ref = others_ref.at[side - 1] if side else own_ref
         for start in range(0, width // 2, block):
             cols = slice(start, start + block)

time: 155 us -> 155 us (level)
  no operation moved by 1% of the time
where the time goes in v6:
time: 155 us; the launch traced here: 154 us
  blocking collectives  59.4 us (38%)
  waiting for transfers between devices  41.1 us (27%)
  starting transfers between devices  26.3 us (17%)
  Pallas kernels  24.6 us (16%)
  local copies, waits for them, and re-layouts  2.44 us (2%)
    all_to_all x2, blocking collectives, exchange(): return lax.all_to_all(value, axis, split_axis=0, concat_axis=0, tiled=True)  59.4 us
    ppermute x6, waiting for transfers between devices, swap(): return lax.ppermute(value, axis, [(0, 1), (1, 0)])  41.1 us
    ppermute x6, starting transfers between devices, swap(): return lax.ppermute(value, axis, [(0, 1), (1, 0)])  16.3 us
    pallas_call x4, Pallas kernels, weigh(): pl.pallas_call(weigh_kernel, grid=(rows // block,), in_specs=[pl.BlockSpe...  14.8 us
    all_to_all x1, starting transfers between devices, exchange(): return lax.all_to_all(value, axis, split_axis=0, concat_axis=0, tiled=True)  9.99 us
    pallas_call x1, Pallas kernels, couple(): pl.pallas_call(couple_kernel, grid_spec=pltpu.PrefetchScalarGridSpec(num_...  6.94 us
  transfers between devices with their start and end apart: 7, of which 1 were waited for; matrix products, arithmetic and copies ran while one was open for 1% of the time, Pallas kernels for 10%

profile of v6, /device:TPU:1, one launch (start us, length us, event | category | flops | bytes accessed | tf_op | source)
XLA Modules:
  0.0 154.0 jit_solution(17611967591780739430)
XLA Ops:
  0.0 36.5 %all_to_all.15.spread_ref = bf16[16,128,256]{2,1,0:T(8,128)(2,1)S(1)} all-to-all(bf16[16,128,256]{2,1,0:T(8,128)(2,1)} %bitcast.18), channel_id=1, replica_groups=mesh['ylo'=2,'z'=8,'xhi'=2,'xlo'=2,'yhi'=4,'core'=2] {'ylo','z'}, dimensions={0} | all-to-all | bytes 2097152 | tf_op jit(solution)/shard_map/all_to_all | solution.py:198
  36.5 0.7 copy-done.3
  37.2 2.1 %pick.1 = bf16[16,2,2,128,128]{4,3,2,1,0:T(8,128)(2,1)} custom-call(s32[2,16]{1,0:T(2,128)S(1)} %copy-done.3, bf16[16,128,256]{2,1,0:T(8,128)(2,1)S(1)} %all_to_all.15.spread_ref), custom_call_target="tpu_custom_call" | custom-call | tf_op jit(solution)/shard_map/pick/pallas_call | solution.py:83
  39.3 10.0 %all-to-all-start.1 = ((bf16[64,128,128]{2,1,0:T(8,128)(2,1)}), bf16[64,128,128]{2,1,0:T(8,128)(2,1)}, u32[]{:S(2)}, u32[]{:S(2)}) async-start(bf16[64,128,128]{2,1,0:T(8,128)(2,1)} %bitcast.29), calls=%async_computation.1 | async-start | bytes 4194304 | tf_op jit(solution)/shard_map/all_to_all | solution.py:198
  49.4 3.3 %collective-permute-start.3 = (bf16[2,1024,256]{2,1,0:T(8,128)(2,1)S(1)}, bf16[2,1024,256]{2,1,0:T(8,128)(2,1)}, u32[]{:S(2)}, u32[]{:S(2)}) collective-permute-start(bf16[2,1024,256]{2,1,0:T(8,128)(2,1)S(1)} %bitcast.19), channel_id=1, source_target_pairs={{0,8},{8,0},{1,9},{9,1},{2,10},{10,2},{3,11},{11,3},{4,12},{12,4},... | collective-permute-start | bytes 3145736 | tf_op jit(solution)/shard_map/ppermute | solution.py:202
  52.6 2.6 %collective-permute-start.1 = (bf16[2,1024,256]{2,1,0:T(8,128)(2,1)S(1)}, bf16[2,1024,256]{2,1,0:T(8,128)(2,1)S(1)}, u32[]{:S(2)}, u32[]{:S(2)}) collective-permute-start(bf16[2,1024,256]{2,1,0:T(8,128)(2,1)S(1)} %bitcast.20), channel_id=1, source_target_pairs={{0,1},{1,0},{2,3},{3,2},{4,5},{5,4},{6,7},{7,6},{8,9},{9,8},{10,11... | collective-permute-start | bytes 3145736 | tf_op jit(solution)/shard_map/ppermute | solution.py:202
  55.2 41.1 %collective-permute-done.3.own_ref = bf16[2,1024,256]{2,1,0:T(8,128)(2,1)} collective-permute-done((bf16[2,1024,256]{2,1,0:T(8,128)(2,1)S(1)}, bf16[2,1024,256]{2,1,0:T(8,128)(2,1)}, u32[]{:S(2)}, u32[]{:S(2)}) %collective-permute-start.3) | collective-permute-done | bytes 1048608 | tf_op jit(solution)/shard_map/ppermute | solution.py:202
  96.3 2.9 %collective-permute-start.5 = (bf16[2,1024,256]{2,1,0:T(8,128)(2,1)}, bf16[2,1024,256]{2,1,0:T(8,128)(2,1)}, u32[]{:S(2)}, u32[]{:S(2)}) collective-permute-start(bf16[2,1024,256]{2,1,0:T(8,128)(2,1)} %collective-permute-done.3.own_ref), channel_id=1, source_target_pairs={{0,1},{1,0},{2,3},{3,2},{4,5},{5,4},{6,7},{7,6},{8,9},{9,8},{10,11... | collective-permute-start | bytes 3145736 | tf_op jit(solution)/shard_map/ppermute | solution.py:202
  99.2 2.6 %collective-permute-start.2 = (bf16[2,3,2,1024]{3,2,1,0:T(2,128)(2,1)S(1)}, bf16[2,3,2,1024]{3,2,1,0:T(2,128)(2,1)S(1)}, u32[]{:S(2)}, u32[]{:S(2)}) collective-permute-start(bf16[2,3,2,1024]{3,2,1,0:T(2,128)(2,1)S(1)} %copy-done.4), channel_id=1, source_target_pairs={{0,8},{8,0},{1,9},{9,1},{2,10},{10,2},{3,11},{11,3},{4,12},{12,4},... | collective-permute-start | bytes 73736 | tf_op jit(solution)/shard_map/ppermute | solution.py:202
  101.8 2.2 %collective-permute-start = (bf16[3,2,1024]{2,1,0:T(2,128)(2,1)S(1)}, bf16[3,2,1024]{2,1,0:T(2,128)(2,1)S(1)}, u32[]{:S(2)}, u32[]{:S(2)}) collective-permute-start(bf16[3,2,1024]{2,1,0:T(2,128)(2,1)S(1)} %get-tuple-element.7), channel_id=1, source_target_pairs={{0,1},{1,0},{2,3},{3,2},{4,5},{5,4},{6,7},{7,6},{8,9},{9,8},{10,11... | collective-permute-start | bytes 36872 | tf_op jit(solution)/shard_map/ppermute | solution.py:202
  104.1 2.8 %collective-permute-start.4 = (bf16[3,2,1024]{2,1,0:T(2,128)(2,1)S(1)}, bf16[3,2,1024]{2,1,0:T(2,128)(2,1)S(1)}, u32[]{:S(2)}, u32[]{:S(2)}) collective-permute-start(bf16[3,2,1024]{2,1,0:T(2,128)(2,1)S(1)} %get-tuple-element.5), channel_id=1, source_target_pairs={{0,1},{1,0},{2,3},{3,2},{4,5},{5,4},{6,7},{7,6},{8,9},{9,8},{10,11... | collective-permute-start | bytes 36872 | tf_op jit(solution)/shard_map/ppermute | solution.py:202
  106.9 0.2 copy.6
  107.1 2.9 %weigh.4 = bf16[2,1024,768]{2,1,0:T(8,128)(2,1)} custom-call(f32[1024,6]{1,0:T(8,128)S(1)} %bitcast.25, bf16[2,1024,256]{2,1,0:T(8,128)(2,1)S(1)} %bitcast.21), custom_call_target="tpu_custom_call" | custom-call | tf_op jit(solution)/shard_map/weigh/pallas_call | solution.py:41
  110.0 0.2 copy.7
  110.3 0.2 copy.8
  110.5 0.0 collective-permute-done.4
  110.5 1.0 copy.9
  111.6 4.4 %weigh.6 = bf16[2,1024,768]{2,1,0:T(8,128)(2,1)} custom-call(f32[1024,6]{1,0:T(8,128)S(1)} %bitcast.24, bf16[2,1024,256]{2,1,0:T(8,128)(2,1)} %collective-permute-done.3.own_ref), custom_call_target="tpu_custom_call" | custom-call | tf_op jit(solution)/shard_map/weigh/pallas_call | solution.py:41
  116.0 2.9 %weigh.5 = bf16[2,1024,768]{2,1,0:T(8,128)(2,1)} custom-call(f32[1024,6]{1,0:T(8,128)S(1)} %bitcast.22, bf16[2,1024,256]{2,1,0:T(8,128)(2,1)S(1)} %collective-permute-done.1.own_ref), custom_call_target="tpu_custom_call" | custom-call | tf_op jit(solution)/shard_map/weigh/pallas_call | solution.py:41
  118.9 0.0 collective-permute-done.5.own_ref
  118.9 4.5 %weigh.7 = bf16[2,1024,768]{2,1,0:T(8,128)(2,1)} custom-call(f32[1024,6]{1,0:T(8,128)S(1)} %bitcast.23, bf16[2,1024,256]{2,1,0:T(8,128)(2,1)} %collective-permute-done.5.own_ref), custom_call_target="tpu_custom_call" | custom-call | tf_op jit(solution)/shard_map/weigh/pallas_call | solution.py:41
  123.5 6.9 %couple.1 = bf16[16,8,1536]{2,1,0:T(8,128)(2,1)S(1)} custom-call(s32[1]{0:T(128)} %bitcast.place_ref, bf16[16,4,128,128]{3,2,1,0:T(8,128)(2,1)} %bitcast.3.fetched_hbm, bf16[2048,768]{1,0:T(8,128)(2,1)S(1)} %bitcast.17, bf16[2048,768]{1,0:T(8,128)(2,1)} %bitcast.27, bf16[2048,768]{1,0:T(8,128)(2,1)} %bitcast.26, bf16[2048,768]{1,0:T(8,128)(2,1)} %bitcast.28), custom_call_target="tpu_custom_call" | custom-call | tf_op jit(solution)/shard_map/couple/pallas_call | solution.py:152
  130.4 22.9 %all_to_all.16.parts_ref = bf16[16,8,1536]{2,1,0:T(8,128)(2,1)S(1)} all-to-all(bf16[16,8,1536]{2,1,0:T(8,128)(2,1)S(1)} %couple.1), channel_id=1, replica_groups=mesh['ylo'=2,'z'=8,'xhi'=2,'xlo'=2,'yhi'=4,'core'=2] {'xhi','yhi','core'}, dimensions={0} | all-to-all | bytes 786432 | tf_op jit(solution)/shard_map/all_to_all | solution.py:198
  153.3 0.7 final.1
  (19 shorter events, 0.1 us)
Async XLA Ops:
  36.5 0.7 copy-start.3
  37.2 12.2 %copy-start.1 = (bf16[1,2,1024,256]{3,2,1,0:T(8,128)(2,1)S(1)}, bf16[1,2,1024,256]{3,2,1,0:T(8,128)(2,1)}, u32[]{:S(2)}) copy-start(bf16[1,2,1024,256]{3,2,1,0:T(8,128)(2,1)} %param.3) | copy-start | bytes 3145732
  37.2 62.0 %copy-start.4 = (bf16[2,3,2,1024]{3,2,1,0:T(2,128)(2,1)S(1)}, bf16[2,3,2,1024]{3,2,1,0:T(2,128)(2,1)}, u32[]{:S(2)}) copy-start(bf16[2,3,2,1024]{3,2,1,0:T(2,128)(2,1)} %param.4) | copy-start | bytes 73732
  39.3 84.1 %all-to-all-start.1 = ((bf16[64,128,128]{2,1,0:T(8,128)(2,1)}), bf16[64,128,128]{2,1,0:T(8,128)(2,1)}, u32[]{:S(2)}, u32[]{:S(2)}) async-start(bf16[64,128,128]{2,1,0:T(8,128)(2,1)} %bitcast.29), calls=%async_computation.1 | async-start | bytes 4194304 | tf_op jit(solution)/shard_map/all_to_all | solution.py:198
  49.4 47.0 %collective-permute-start.3 = (bf16[2,1024,256]{2,1,0:T(8,128)(2,1)S(1)}, bf16[2,1024,256]{2,1,0:T(8,128)(2,1)}, u32[]{:S(2)}, u32[]{:S(2)}) collective-permute-start(bf16[2,1024,256]{2,1,0:T(8,128)(2,1)S(1)} %bitcast.19), channel_id=1, source_target_pairs={{0,8},{8,0},{1,9},{9,1},{2,10},{10,2},{3,11},{11,3},{4,12},{12,4},... | collective-permute-start | bytes 3145736 | tf_op jit(solution)/shard_map/ppermute | solution.py:202
  52.6 63.4 %collective-permute-start.1 = (bf16[2,1024,256]{2,1,0:T(8,128)(2,1)S(1)}, bf16[2,1024,256]{2,1,0:T(8,128)(2,1)S(1)}, u32[]{:S(2)}, u32[]{:S(2)}) collective-permute-start(bf16[2,1024,256]{2,1,0:T(8,128)(2,1)S(1)} %bitcast.20), channel_id=1, source_target_pairs={{0,1},{1,0},{2,3},{3,2},{4,5},{5,4},{6,7},{7,6},{8,9},{9,8},{10,11... | collective-permute-start | bytes 3145736 | tf_op jit(solution)/shard_map/ppermute | solution.py:202
  96.3 22.6 %collective-permute-start.5 = (bf16[2,1024,256]{2,1,0:T(8,128)(2,1)}, bf16[2,1024,256]{2,1,0:T(8,128)(2,1)}, u32[]{:S(2)}, u32[]{:S(2)}) collective-permute-start(bf16[2,1024,256]{2,1,0:T(8,128)(2,1)} %collective-permute-done.3.own_ref), channel_id=1, source_target_pairs={{0,1},{1,0},{2,3},{3,2},{4,5},{5,4},{6,7},{7,6},{8,9},{9,8},{10,11... | collective-permute-start | bytes 3145736 | tf_op jit(solution)/shard_map/ppermute | solution.py:202
  99.2 4.8 %collective-permute-start.2 = (bf16[2,3,2,1024]{3,2,1,0:T(2,128)(2,1)S(1)}, bf16[2,3,2,1024]{3,2,1,0:T(2,128)(2,1)S(1)}, u32[]{:S(2)}, u32[]{:S(2)}) collective-permute-start(bf16[2,3,2,1024]{3,2,1,0:T(2,128)(2,1)S(1)} %copy-done.4), channel_id=1, source_target_pairs={{0,8},{8,0},{1,9},{9,1},{2,10},{10,2},{3,11},{11,3},{4,12},{12,4},... | collective-permute-start | bytes 73736 | tf_op jit(solution)/shard_map/ppermute | solution.py:202
  101.8 8.2 %collective-permute-start = (bf16[3,2,1024]{2,1,0:T(2,128)(2,1)S(1)}, bf16[3,2,1024]{2,1,0:T(2,128)(2,1)S(1)}, u32[]{:S(2)}, u32[]{:S(2)}) collective-permute-start(bf16[3,2,1024]{2,1,0:T(2,128)(2,1)S(1)} %get-tuple-element.7), channel_id=1, source_target_pairs={{0,1},{1,0},{2,3},{3,2},{4,5},{5,4},{6,7},{7,6},{8,9},{9,8},{10,11... | collective-permute-start | bytes 36872 | tf_op jit(solution)/shard_map/ppermute | solution.py:202
  104.1 6.4 %collective-permute-start.4 = (bf16[3,2,1024]{2,1,0:T(2,128)(2,1)S(1)}, bf16[3,2,1024]{2,1,0:T(2,128)(2,1)S(1)}, u32[]{:S(2)}, u32[]{:S(2)}) collective-permute-start(bf16[3,2,1024]{2,1,0:T(2,128)(2,1)S(1)} %get-tuple-element.5), channel_id=1, source_target_pairs={{0,1},{1,0},{2,3},{3,2},{4,5},{5,4},{6,7},{7,6},{8,9},{9,8},{10,11... | collective-permute-start | bytes 36872 | tf_op jit(solution)/shard_map/ppermute | solution.py:202
  116.0 2.9 %copy-start.2 = (f32[6,1024]{0,1:T(8,128)S(1)}, f32[6,1024]{0,1:T(8,128)}, u32[]{:S(2)}) copy-start(f32[6,1024]{0,1:T(8,128)} %copy.9) | copy-start | bytes 73732
  118.9 4.5 %copy-start = (bf16[2,1024,768]{2,1,0:T(8,128)(2,1)S(1)}, bf16[2,1024,768]{2,1,0:T(8,128)(2,1)}, u32[]{:S(2)}) copy-start(bf16[2,1024,768]{2,1,0:T(8,128)(2,1)} %weigh.4) | copy-start | bytes 9437188
